TPU v7x, 32 devices: a whole 2x2x4 slice. The times are simulated.
32 devices in a mesh: rows: 8 (over z, x), seq: 4 (over y, core).
Axes of the slice: x: 2, y: 2, z: 4, core: 2. Of those that a mesh axis runs over, the one named last changes fastest.
Arguments:
- inputs: bfloat16 [8, 2048, 1024], P('rows', 'seq'), may hold values from -6 to 6
- skip_feats: bfloat16 [8, 2048, 1024], P('rows', 'seq'), may hold values from -6 to 6
- seg_ids: int32 [8, 2048], P('rows'), may hold values from 0 to 5, never falling along the last dimension, each value on 1 to 682 neighbouring positions
- frame_valid: int32 [8, 2048], P('rows'), may hold values 0 or 1
- w_skip: bfloat16 [2048, 1024], replicated, may hold values from -0.125 to 0.125
- gain_one: bfloat16 [1024], replicated, may hold values from 0.5 to 1.5
- w_qkv: bfloat16 [1024, 3072], replicated, may hold values from -0.1875 to 0.1875
- w_out: bfloat16 [1024, 1024], replicated, may hold values from -0.5 to 0.5
- gain_two: bfloat16 [1024], replicated, may hold values from 0.5 to 1.5
- w_up: bfloat16 [1024, 4096], replicated, may hold values from -0.1875 to 0.1875
- b_up: bfloat16 [4096], replicated, may hold values from -3 to 3
- w_down: bfloat16 [4096, 1024], replicated, may hold values from -0.09375 to 0.09375
- b_down: bfloat16 [1024], replicated, may hold values from -2 to 2
- cotangent: bfloat16 [8, 2048, 1024], P('rows', 'seq'), may hold values from -6 to 6
Outputs:
- output: bfloat16 [8, 2048, 1024], P('rows', 'seq')
- input_grad: bfloat16 [8, 2048, 1024], P('rows', 'seq')
- skip_grad: bfloat16 [8, 2048, 1024], P('rows', 'seq')
- w_skip_grad: float32 [2048, 1024], P(('rows', 'seq'))
- gain_one_grad: float32 [1024], P(('rows', 'seq'))
- w_qkv_grad: float32 [1024, 3072], P(('rows', 'seq'))
- w_out_grad: float32 [1024, 1024], P(('rows', 'seq'))
- gain_two_grad: float32 [1024], P(('rows', 'seq'))
- w_up_grad: float32 [1024, 4096], P(('rows', 'seq'))
- b_up_grad: float32 [4096], P(('rows', 'seq'))
- w_down_grad: float32 [4096, 1024], P(('rows', 'seq'))
- b_down_grad: float32 [1024], P(('rows', 'seq'))
Inputs may be any that keep to these rules, and one draw needn't show every extreme that they name: `seg_ids`: in each row the segment numbers never fall along the frames; every segment has 1 to 682 frames and one has exactly 682.
All inputs are finite; a program needn't handle non-finite values. No bound on the sum of `frame_valid` on one device may be relied on, other than what follows from the above.
Results may differ from a plain program's by a relative error of at most 0.015.
Values may be sent and summed in bfloat16 or wider, within the bound.
A program may use at most 192 MiB of HBM per device.

v0:
```python
import math

import jax
import jax.numpy as jnp
from jax import lax
from jax.sharding import PartitionSpec as P

D = 1024
H = 16
HD = 64


epsilon = 1e-05


def norm_forward(value, gain_vec):
    center = value - jnp.mean(value, axis=-1, keepdims=True)
    spread = jnp.mean(center * center, axis=-1, keepdims=True)
    inverse = lax.rsqrt(spread + epsilon)
    unit = center * inverse
    return (unit, inverse, unit * gain_vec)


def norm_backward(upstream, unit, inverse, gain_vec):
    scaled = upstream * gain_vec
    gain_grad = jnp.sum(upstream * unit, axis=(0, 1))
    inner = (
        scaled
        - jnp.mean(scaled, axis=-1, keepdims=True)
        - unit * jnp.mean(scaled * unit, axis=-1, keepdims=True)
    )
    return (inverse * inner, gain_grad)


def gelu_exact(value):
    return jax.nn.gelu(value, approximate=False)


def block_scores(q_blk, pos_blk, seg_blk, all_keys, seg_row, valid_row, slopes, score_scale):
    key_pos = jnp.arange(all_keys.shape[0])
    scores = (
        jnp.einsum("qhd,khd->hqk", q_blk, all_keys, preferred_element_type=jnp.float32)
        * score_scale
    )
    distance = jnp.abs(pos_blk[:, None] - key_pos[None, :]).astype(jnp.float32)
    scores = scores - slopes[:, None, None] * distance[None]
    allowed = (seg_blk[:, None] == seg_row[None, :]) & (
        (valid_row[None, :] == 1) | (pos_blk[:, None] == key_pos[None, :])
    )
    return jnp.where(allowed[None], scores, -jnp.inf)


def split_row(packed_row, heads_local):
    length = packed_row.shape[0]
    qkv_rows = packed_row.reshape(length, 3, heads_local, HD)
    return (qkv_rows[:, 0], qkv_rows[:, 1], qkv_rows[:, 2])


def attend_row(packed_row, seg_row, valid_row, slopes, heads_local, block_rows, score_scale):
    length = packed_row.shape[0]
    queries, all_keys, all_values = split_row(packed_row, heads_local)
    count = length // block_rows
    positions = jnp.arange(length)

    def one_block(block_in):
        q_blk, pos_blk, seg_blk = block_in
        scores = block_scores(
            q_blk, pos_blk, seg_blk, all_keys, seg_row, valid_row, slopes, score_scale
        )
        peak = jnp.max(scores, axis=-1, keepdims=True)
        log_total = peak + jnp.log(jnp.sum(jnp.exp(scores - peak), axis=-1, keepdims=True))
        attn_probs = jnp.exp(scores - log_total).astype(jnp.bfloat16)
        attended = jnp.einsum(
            "hqk,khd->qhd", attn_probs, all_values, preferred_element_type=jnp.float32
        )
        return (attended.astype(jnp.bfloat16), log_total[..., 0])

    attended, log_total = lax.map(
        one_block,
        (
            queries.reshape(count, block_rows, heads_local, HD),
            positions.reshape(count, block_rows),
            seg_row.reshape(count, block_rows),
        ),
    )
    return (attended.reshape(length, 1, heads_local * HD), log_total)


def attend_row_back(
    packed_row,
    log_total,
    grad_row,
    seg_row,
    valid_row,
    slopes,
    heads_local,
    block_rows,
    score_scale,
):
    length = packed_row.shape[0]
    queries, all_keys, all_values = split_row(packed_row, heads_local)
    count = length // block_rows
    positions = jnp.arange(length)
    grad_out = grad_row.reshape(count, block_rows, heads_local, HD)

    def one_block(carry, block_in):
        key_grad, value_grad = carry
        q_blk, pos_blk, seg_blk, total_blk, grad_blk = block_in
        scores = block_scores(
            q_blk, pos_blk, seg_blk, all_keys, seg_row, valid_row, slopes, score_scale
        )
        soft = jnp.exp(scores - total_blk[..., None])
        value_grad = value_grad + jnp.einsum(
            "hqk,qhd->khd", soft.astype(jnp.bfloat16), grad_blk, preferred_element_type=jnp.float32
        )
        prob_grad = jnp.einsum(
            "qhd,khd->hqk", grad_blk, all_values, preferred_element_type=jnp.float32
        )
        score_grad = (
            soft * (prob_grad - jnp.sum(soft * prob_grad, axis=-1, keepdims=True))
        ).astype(jnp.bfloat16)
        query_grad = (
            jnp.einsum("hqk,khd->qhd", score_grad, all_keys, preferred_element_type=jnp.float32)
            * score_scale
        )
        key_grad = (
            key_grad
            + jnp.einsum("hqk,qhd->khd", score_grad, q_blk, preferred_element_type=jnp.float32)
            * score_scale
        )
        return ((key_grad, value_grad), query_grad)

    zero_rows = jnp.zeros((length, heads_local, HD), jnp.float32)
    (key_grad, value_grad), query_grad = lax.scan(
        one_block,
        (zero_rows, zero_rows),
        (
            queries.reshape(count, block_rows, heads_local, HD),
            positions.reshape(count, block_rows),
            seg_row.reshape(count, block_rows),
            log_total,
            grad_out,
        ),
    )
    stacked = jnp.stack([query_grad.reshape(length, heads_local, HD), key_grad, value_grad], axis=1)
    return stacked.astype(jnp.bfloat16).reshape(length, 3, 1, heads_local * HD)


def body(
    inputs,
    skip_feats,
    seg_ids,
    frame_valid,
    w_skip,
    gain_one,
    w_qkv,
    w_out,
    gain_two,
    w_up,
    b_up,
    w_down,
    b_down,
    cotangent,
):
    parts = lax.axis_size("seq")
    heads_local = H // parts
    width_local = heads_local * HD
    rows_here = inputs.shape[0]
    frames = inputs.shape[1]
    length = frames * parts
    block_rows = min(512, length)
    score_scale = 1.0 / math.sqrt(HD)
    first_head = lax.axis_index("seq") * heads_local
    slopes = jnp.exp2(-8.0 * (first_head + jnp.arange(heads_local) + 1).astype(jnp.float32) / H)
    gain_first = gain_one.astype(jnp.float32)
    gain_second = gain_two.astype(jnp.float32)
    bias_up = b_up.astype(jnp.float32)
    joined = jnp.concatenate([inputs, skip_feats], axis=-1)
    stem_out = jnp.einsum("rfc,cd->rfd", joined, w_skip, preferred_element_type=jnp.float32)
    unit_one, inverse_one, normed = norm_forward(stem_out, gain_first)
    normed = normed.astype(jnp.bfloat16)
    packed = jnp.einsum("rfd,de->rfe", normed, w_qkv, preferred_element_type=jnp.float32).astype(
        jnp.bfloat16
    )
    packed = packed.reshape(rows_here, frames, 3, parts, width_local)
    by_heads = lax.all_to_all(packed, "seq", split_axis=3, concat_axis=1, tiled=True)

    def forward_row(row_data):
        return attend_row(
            row_data[0], row_data[1], row_data[2], slopes, heads_local, block_rows, score_scale
        )

    attended, log_total = lax.map(forward_row, (by_heads, seg_ids, frame_valid))
    by_frames = lax.all_to_all(attended, "seq", split_axis=1, concat_axis=2, tiled=True)
    mixed_out = by_frames.reshape(rows_here, frames, D)
    middle = stem_out + jnp.einsum(
        "rfd,de->rfe", mixed_out, w_out, preferred_element_type=jnp.float32
    )
    unit_two, inverse_two, second = norm_forward(middle, gain_second)
    second = second.astype(jnp.bfloat16)
    hidden = jnp.einsum("rfd,dk->rfk", second, w_up, preferred_element_type=jnp.float32) + bias_up
    active_full, gelu_back = jax.vjp(gelu_exact, hidden)
    active = active_full.astype(jnp.bfloat16)
    result = (
        middle
        + jnp.einsum("rfk,kd->rfd", active, w_down, preferred_element_type=jnp.float32)
        + b_down.astype(jnp.float32)
    )
    output = result.astype(jnp.bfloat16)
    cot_full = cotangent.astype(jnp.float32)
    down_grad = jnp.einsum("rfk,rfd->kd", active, cotangent, preferred_element_type=jnp.float32)
    bias_down_grad = jnp.sum(cot_full, axis=(0, 1))
    active_grad = jnp.einsum("rfd,kd->rfk", cotangent, w_down, preferred_element_type=jnp.float32)
    hidden_grad = gelu_back(active_grad)[0].astype(jnp.bfloat16)
    up_grad = jnp.einsum("rfd,rfk->dk", second, hidden_grad, preferred_element_type=jnp.float32)
    bias_up_grad = jnp.sum(hidden_grad.astype(jnp.float32), axis=(0, 1))
    second_grad = jnp.einsum("rfk,dk->rfd", hidden_grad, w_up, preferred_element_type=jnp.float32)
    middle_part, gain_two_grad = norm_backward(second_grad, unit_two, inverse_two, gain_second)
    middle_grad = cot_full + middle_part
    middle_low = middle_grad.astype(jnp.bfloat16)
    out_grad = jnp.einsum("rfd,rfe->de", mixed_out, middle_low, preferred_element_type=jnp.float32)
    mixed_grad = jnp.einsum(
        "rfe,de->rfd", middle_low, w_out, preferred_element_type=jnp.float32
    ).astype(jnp.bfloat16)
    grad_heads = lax.all_to_all(
        mixed_grad.reshape(rows_here, frames, parts, width_local),
        "seq",
        split_axis=2,
        concat_axis=1,
        tiled=True,
    )

    def backward_row(row_data):
        return attend_row_back(
            row_data[0],
            row_data[1],
            row_data[2],
            row_data[3],
            row_data[4],
            slopes,
            heads_local,
            block_rows,
            score_scale,
        )

    packed_grad = lax.map(backward_row, (by_heads, log_total, grad_heads, seg_ids, frame_valid))
    packed_back = lax.all_to_all(packed_grad, "seq", split_axis=1, concat_axis=3, tiled=True)
    packed_back = packed_back.reshape(rows_here, frames, 3 * D)
    qkv_grad = jnp.einsum("rfd,rfe->de", normed, packed_back, preferred_element_type=jnp.float32)
    normed_grad = jnp.einsum("rfe,de->rfd", packed_back, w_qkv, preferred_element_type=jnp.float32)
    stem_part, gain_one_grad = norm_backward(normed_grad, unit_one, inverse_one, gain_first)
    stem_low = (middle_grad + stem_part).astype(jnp.bfloat16)
    skip_w_grad = jnp.einsum("rfc,rfd->cd", joined, stem_low, preferred_element_type=jnp.float32)
    joined_grad = jnp.einsum("rfd,cd->rfc", stem_low, w_skip, preferred_element_type=jnp.float32)
    input_grad = joined_grad[..., :D].astype(jnp.bfloat16)
    skip_grad = joined_grad[..., D:].astype(jnp.bfloat16)
    (
        skip_share,
        gain_one_share,
        qkv_share,
        out_share,
        gain_two_share,
        up_share,
        bias_up_share,
        down_share,
        bias_down_share,
    ) = (
        lax.psum_scatter(skip_w_grad, ("rows", "seq"), scatter_dimension=0, tiled=True),
        lax.psum_scatter(gain_one_grad, ("rows", "seq"), scatter_dimension=0, tiled=True),
        lax.psum_scatter(qkv_grad, ("rows", "seq"), scatter_dimension=0, tiled=True),
        lax.psum_scatter(out_grad, ("rows", "seq"), scatter_dimension=0, tiled=True),
        lax.psum_scatter(gain_two_grad, ("rows", "seq"), scatter_dimension=0, tiled=True),
        lax.psum_scatter(up_grad, ("rows", "seq"), scatter_dimension=0, tiled=True),
        lax.psum_scatter(bias_up_grad, ("rows", "seq"), scatter_dimension=0, tiled=True),
        lax.psum_scatter(down_grad, ("rows", "seq"), scatter_dimension=0, tiled=True),
        lax.psum_scatter(bias_down_grad, ("rows", "seq"), scatter_dimension=0, tiled=True),
    )
    return (
        output,
        input_grad,
        skip_grad,
        skip_share,
        gain_one_share,
        qkv_share,
        out_share,
        gain_two_share,
        up_share,
        bias_up_share,
        down_share,
        bias_down_share,
    )


def solution(mesh):
    return jax.shard_map(
        body,
        mesh=mesh,
        in_specs=(
            P("rows", "seq", None),
            P("rows", "seq", None),
            P("rows", None),
            P("rows", None),
            P(),
            P(),
            P(),
            P(),
            P(),
            P(),
            P(),
            P(),
            P(),
            P("rows", "seq", None),
        ),
        out_specs=(
            P("rows", "seq", None),
            P("rows", "seq", None),
            P("rows", "seq", None),
            P(("rows", "seq"), None),
            P(("rows", "seq")),
            P(("rows", "seq"), None),
            P(("rows", "seq"), None),
            P(("rows", "seq")),
            P(("rows", "seq"), None),
            P(("rows", "seq")),
            P(("rows", "seq"), None),
            P(("rows", "seq")),
        ),
        check_vma=False,
    )
```

profile of v0, /device:TPU:0, one launch (start us, length us, event | category | flops | bytes accessed | tf_op | source)
XLA Modules:
  0.0 1325.0 jit_solution(4575809649064550022)
XLA Ops:
  7.2 5.4 fusion.74
  14.6 5.2 convolution_convert_fusion
  19.8 6.7 reshape.605
  36.5 36.4 %all-to-all-done = bf16[1,512,3,4,256]{4,1,2,0,3:T(8,128)(2,1)} async-done(((bf16[1,512,3,4,256]{4,1,2,0,3:T(8,128)(2,1)}), bf16[1,512,3,4,256]{4,1,2,0,3:T(8,128)(2,1)}, u32[]{:S(2)}, u32[]{:S(2)}) %all-to-all-start) | async-done | bytes 3145760 | tf_op jit(solution)/shard_map/all_to_all | solution.py:186
  72.9 6.2 copy.64
  79.1 6.1 reshape.606
  91.9 90.6 %while.46 = (s32[]{:T(128)}, bf16[4,512,4,64]{1,3,2,0:T(8,128)(2,1)}, f32[4,4,512]{2,1,0:T(4,128)S(1)}, s32[4,512]{1,0:T(4,128)S(1)}, s32[2048]{0:T(1024)S(1)}, ...) while((s32[]{:T(128)}, ...), condition=%wide.region_5.6_spmd.clone, body=%wide.region_2.5_spmd.clone.sunk | while | flops 1152516096 | bytes 99192080 | solution.py:78
  94.4 6.3 fusion.125
  100.7 5.8 exponential_reduce_fusion.2
  106.5 8.1 fusion.126
  117.0 6.3 fusion.125
  123.3 5.8 exponential_reduce_fusion.2
  129.1 8.2 fusion.126
  139.6 6.3 fusion.125
  145.9 5.8 exponential_reduce_fusion.2
  151.7 8.2 fusion.126
  162.2 6.3 fusion.125
  168.5 5.8 exponential_reduce_fusion.2
  174.3 8.2 fusion.126
  186.6 8.2 reshape.615
  195.3 12.0 reduce.26
  212.6 14.4 %all-to-all-done.1 = bf16[4,2,65536]{2,1,0:T(2,128)(2,1)S(1)} async-done(((bf16[4,2,65536]{2,1,0:T(2,128)(2,1)}), bf16[4,2,65536]{2,1,0:T(2,128)(2,1)S(1)}, u32[]{:S(2)}, u32[]{:S(2)}) %all-to-all-start.1) | async-done | bytes 1048608 | tf_op jit(solution)/shard_map/all_to_all | solution.py:194
  236.9 27.8 %multiply_convert_fusion.1 = (bf16[512,4096]{1,0:T(8,128)(2,1)}, f32[512,4096]{1,0:T(8,128)}, f32[512,4096]{1,0:T(8,128)}) fusion(f32[4096]{0:T(1024)S(1)} %convert_element_type.104, bf16[1024,4096]{1,0:T(8,128)(2,1)} %param.27, f32[512,1024]{1,0:T(8,128)S(1)} %get-tuple-element.449, f32[1024]{0:T(1024)S(1)} %convert_element_type.102, ...), kind=kOutput, calls=%fused_computation.65 | convolution fusion | flops 4435476480 | bytes 31481856 | tf_op jit(solution)/shard_map/rfd,dk->rfk/dot_general | solution.py:201
  264.7 14.0 %convert_reduce_fusion = (f32[4096]{0:T(1024)}, bf16[512,4096]{1,0:T(8,128)(2,1)S(1)}) fusion(f32[512,4096]{1,0:T(8,128)} %get-tuple-element.430, bf16[4096,1024]{1,0:T(8,128)(2,1)} %param.29, bf16[1,512,1024]{2,1,0:T(8,128)(2,1)S(1)} %copy-done.18, f32[512,4096]{1,0:T(8,128)} %get-tuple-element.450, f32[4096]{0:T(1024)S(1)} %convert_element_type.104), kind=kOutput, calls=%fused_computation.63 | convolution fusion | flops 4330614784 | bytes 30441472 | tf_op jit(solution)/shard_map/rfd,kd->rfk/dot_general | solution.py:213
  278.7 9.6 multiply_reduce_fusion.1
  306.2 11.1 all-to-all-done.2
  319.6 236.3 %while.47 = (s32[]{:T(128)}, f32[2048,4,64]{0,2,1:T(8,128)}, f32[2048,4,64]{0,2,1:T(8,128)}, bf16[4,512,4,64]{1,3,2,0:T(8,128)(2,1)}, bf16[4,512,4,64]{1,3,2,0:T...) while((s32[]{:T(128)}, f32[2048,4,64]{0,2,1:T(8,128)}, ...), condition=%wide.region_12.13_spmd.clone, body=%wide.region_10.12_spmd.clone.sunk | while | flops 2740584448 | bytes 224997680 | solution.py:134
  321.1 9.1 fusion.136
  331.0 14.0 %multiply_reduce_fusion.10 = (f32[4,512]{1,0:T(4,128)S(1)}, f32[4,512,2048]{2,1,0:T(8,128)}) fusion(f32[4,512,2048]{2,1,0:T(8,128)} %fusion.136, f32[4,512]{1,0:T(4,128)S(1)} %dynamic-slice_bitcast_fusion.2, f32[512,2048]{1,0:T(8,128)S(1)} %abs_convert_fusion.5, f32[4]{0:T(128)S(1)} %multiply_exponential_fusion.5, ...), kind=kOutput, calls=%fused_computation.27.clone.1 | convolution fusion | flops 566228992 | bytes 40124944 | tf_op jit(solution)/shard_map/while/body/eval_jaxpr/while/body/eval_jaxpr/qhd,khd->hqk/dot_general | solution.py:42
  345.0 15.1 %multiply_convert_fusion.9 = bf16[4,512,2048]{2,1,0:T(8,128)(2,1)} fusion(f32[4,512,2048]{2,1,0:T(8,128)} %get-tuple-element.627, f32[4,512,2048]{2,1,0:T(8,128)} %fusion.136, f32[4,512]{1,0:T(4,128)S(1)} %get-tuple-element.628), kind=kLoop, calls=%fused_computation.26.clone.1 | loop fusion | flops 12582912 | bytes 41951232 | tf_op jit(solution)/shard_map/while/body/eval_jaxpr/while/body/eval_jaxpr/convert_element_type | solution.py:121
  360.0 6.6 fusion.138
  366.6 6.8 fusion.140
  379.1 9.1 fusion.136
  388.9 14.0 %multiply_reduce_fusion.10 = (f32[4,512]{1,0:T(4,128)S(1)}, f32[4,512,2048]{2,1,0:T(8,128)}) fusion(f32[4,512,2048]{2,1,0:T(8,128)} %fusion.136, f32[4,512]{1,0:T(4,128)S(1)} %dynamic-slice_bitcast_fusion.2, f32[512,2048]{1,0:T(8,128)S(1)} %abs_convert_fusion.5, f32[4]{0:T(128)S(1)} %multiply_exponential_fusion.5, ...), kind=kOutput, calls=%fused_computation.27.clone.1 | convolution fusion | flops 566228992 | bytes 40124944 | tf_op jit(solution)/shard_map/while/body/eval_jaxpr/while/body/eval_jaxpr/qhd,khd->hqk/dot_general | solution.py:42
  402.9 15.1 %multiply_convert_fusion.9 = bf16[4,512,2048]{2,1,0:T(8,128)(2,1)} fusion(f32[4,512,2048]{2,1,0:T(8,128)} %get-tuple-element.627, f32[4,512,2048]{2,1,0:T(8,128)} %fusion.136, f32[4,512]{1,0:T(4,128)S(1)} %get-tuple-element.628), kind=kLoop, calls=%fused_computation.26.clone.1 | loop fusion | flops 12582912 | bytes 41951232 | tf_op jit(solution)/shard_map/while/body/eval_jaxpr/while/body/eval_jaxpr/convert_element_type | solution.py:121
  418.0 7.2 fusion.138
  425.2 6.8 fusion.140
  432.0 5.0 fusion.139
  438.5 9.1 fusion.136
  448.4 14.0 %multiply_reduce_fusion.10 = (f32[4,512]{1,0:T(4,128)S(1)}, f32[4,512,2048]{2,1,0:T(8,128)}) fusion(f32[4,512,2048]{2,1,0:T(8,128)} %fusion.136, f32[4,512]{1,0:T(4,128)S(1)} %dynamic-slice_bitcast_fusion.2, f32[512,2048]{1,0:T(8,128)S(1)} %abs_convert_fusion.5, f32[4]{0:T(128)S(1)} %multiply_exponential_fusion.5, ...), kind=kOutput, calls=%fused_computation.27.clone.1 | convolution fusion | flops 566228992 | bytes 40124944 | tf_op jit(solution)/shard_map/while/body/eval_jaxpr/while/body/eval_jaxpr/qhd,khd->hqk/dot_general | solution.py:42
  462.4 15.0 %multiply_convert_fusion.9 = bf16[4,512,2048]{2,1,0:T(8,128)(2,1)} fusion(f32[4,512,2048]{2,1,0:T(8,128)} %get-tuple-element.627, f32[4,512,2048]{2,1,0:T(8,128)} %fusion.136, f32[4,512]{1,0:T(4,128)S(1)} %get-tuple-element.628), kind=kLoop, calls=%fused_computation.26.clone.1 | loop fusion | flops 12582912 | bytes 41951232 | tf_op jit(solution)/shard_map/while/body/eval_jaxpr/while/body/eval_jaxpr/convert_element_type | solution.py:121
  477.3 7.2 fusion.138
  484.5 6.8 fusion.140
  491.3 5.0 fusion.139
  497.8 9.1 fusion.136
  507.7 13.9 %multiply_reduce_fusion.10 = (f32[4,512]{1,0:T(4,128)S(1)}, f32[4,512,2048]{2,1,0:T(8,128)}) fusion(f32[4,512,2048]{2,1,0:T(8,128)} %fusion.136, f32[4,512]{1,0:T(4,128)S(1)} %dynamic-slice_bitcast_fusion.2, f32[512,2048]{1,0:T(8,128)S(1)} %abs_convert_fusion.5, f32[4]{0:T(128)S(1)} %multiply_exponential_fusion.5, ...), kind=kOutput, calls=%fused_computation.27.clone.1 | convolution fusion | flops 566228992 | bytes 40124944 | tf_op jit(solution)/shard_map/while/body/eval_jaxpr/while/body/eval_jaxpr/qhd,khd->hqk/dot_general | solution.py:42
  521.6 15.0 %multiply_convert_fusion.9 = bf16[4,512,2048]{2,1,0:T(8,128)(2,1)} fusion(f32[4,512,2048]{2,1,0:T(8,128)} %get-tuple-element.627, f32[4,512,2048]{2,1,0:T(8,128)} %fusion.136, f32[4,512]{1,0:T(4,128)S(1)} %get-tuple-element.628), kind=kLoop, calls=%fused_computation.26.clone.1 | loop fusion | flops 12582912 | bytes 41951232 | tf_op jit(solution)/shard_map/while/body/eval_jaxpr/while/body/eval_jaxpr/convert_element_type | solution.py:121
  536.6 7.2 fusion.138
  543.8 6.8 fusion.140
  550.6 5.0 fusion.139
  563.8 7.2 copy.73
  570.9 51.9 %all_to_all.60 = bf16[1,2048,3,1,256]{4,2,3,0,1:T(4,128)(2,1)S(1)} all-to-all(bf16[1,2048,3,1,256]{4,2,3,0,1:T(4,128)(2,1)} %copy.73), channel_id=1, replica_groups=mesh['rows'=8,'seq'=4] {'seq'}, dimensions={1} | all-to-all | bytes 6291456 | tf_op jit(solution)/shard_map/all_to_all | solution.py:247
  624.9 4.8 copy.75
  629.8 8.6 fusion.69
  638.5 8.6 multiply_reduce_fusion.2
  648.9 5.7 fusion.53
  656.3 11.3 fusion.70
  668.9 11.1 fusion.59
  680.7 10.9 fusion.52
  691.6 45.8 %all-reduce.4 = (f32[1024]{0:T(1024)S(1)}, f32[1024]{0:T(1024)S(1)}, f32[4096]{0:T(1024)S(1)}, f32[1024]{0:T(1024)S(1)}) all-reduce(f32[1024]{0:T(1024)S(1)} %get-tuple-element.369, f32[1024]{0:T(1024)S(1)} %copy-done.41, f32[4096]{0:T(1024)S(1)} %copy-done.35, ...), channel_id=3, replica_groups=mesh['rows'=8,'seq'=4] {'rows','seq'}, use_global_device_ids=true, to_apply=%region_17.18.clone | all-reduce | flops 7168 | bytes 57344
  746.0 51.8 %reduce-scatter.8.cloned.1.call-done = f32[32,3072]{1,0:T(8,128)} async-done(((f32[1024,3072]{1,0:T(8,128)}), f32[32,3072]{1,0:T(8,128)}) %reduce-scatter.8.cloned.1.call-update) | async-done | bytes 393232 | tf_op jit(solution)/shard_map/reduce_scatter | solution.py:270
  797.8 151.3 %reduce-scatter.6.cloned.1.call-done = f32[64,1024]{1,0:T(8,128)} async-done(((f32[2048,1024]{1,0:T(8,128)}), f32[64,1024]{1,0:T(8,128)}) %reduce-scatter.6.cloned.1.call-update) | async-done | bytes 262160 | tf_op jit(solution)/shard_map/reduce_scatter | solution.py:268
  949.1 181.7 %reduce-scatter.12.cloned.1.call-done = f32[32,4096]{1,0:T(8,128)} async-done(((f32[1024,4096]{1,0:T(8,128)}), f32[32,4096]{1,0:T(8,128)}) %reduce-scatter.12.cloned.1.call-update) | async-done | bytes 524304 | tf_op jit(solution)/shard_map/reduce_scatter | solution.py:273
  1130.9 187.4 %reduce-scatter.14.cloned.1.call-done = f32[128,1024]{1,0:T(8,128)} async-done(((f32[4096,1024]{1,0:T(8,128)}), f32[128,1024]{1,0:T(8,128)}) %reduce-scatter.14.cloned.1.call-update) | async-done | bytes 524304 | tf_op jit(solution)/shard_map/reduce_scatter | solution.py:275
  (249 shorter events, 104.5 us)
Async XLA Ops:
  7.2 226.4 %copy-start = (bf16[1024,1024]{1,0:T(8,128)(2,1)S(1)}, bf16[1024,1024]{1,0:T(8,128)(2,1)}, u32[]{:S(2)}) copy-start(bf16[1024,1024]{1,0:T(8,128)(2,1)} %param.25) | copy-start | bytes 6291460
  7.2 5.8 copy-start.42
  7.2 7.4 copy-start.45
  30.5 5.3 copy-start.24
  30.5 42.4 %all-to-all-start = ((bf16[1,512,3,4,256]{4,1,2,0,3:T(8,128)(2,1)}), bf16[1,512,3,4,256]{4,1,2,0,3:T(8,128)(2,1)}, u32[]{:S(2)}, u32[]{:S(2)}) async-start(bf16[1,512,3,4,256]{4,1,2,0,3:T(8,128)(2,1)} %copy.63), calls=%async_computation | async-start | bytes 6291456 | tf_op jit(solution)/shard_map/all_to_all | solution.py:186
  85.2 6.7 copy-start.25
  92.1 2.3 copy-start.4
  93.6 7.1 copy-start.6
  94.4 6.3 copy-start.3
  114.7 2.3 copy-start.4
  116.2 7.1 copy-start.6
  117.0 6.3 copy-start.3
  137.3 2.3 copy-start.4
  138.8 7.1 copy-start.6
  139.6 6.3 copy-start.3
  159.9 2.3 copy-start.4
  161.4 7.1 copy-start.6
  162.2 6.3 copy-start.3
  194.8 17.7 %copy-start.43 = (bf16[1024]{0:T(1024)(128)(2,1)S(1)}, bf16[1024]{0:T(1024)(128)(2,1)}, u32[]{:S(2)}) copy-start(bf16[1024]{0:T(1024)(128)(2,1)} %param.26) | copy-start | bytes 6148
  194.8 17.8 %copy-start.38 = (bf16[4096]{0:T(1024)(128)(2,1)S(1)}, bf16[4096]{0:T(1024)(128)(2,1)}, u32[]{:S(2)}) copy-start(bf16[4096]{0:T(1024)(128)(2,1)} %param.28) | copy-start | bytes 24580
  209.0 18.0 %all-to-all-start.1 = ((bf16[4,2,65536]{2,1,0:T(2,128)(2,1)}), bf16[4,2,65536]{2,1,0:T(2,128)(2,1)S(1)}, u32[]{:S(2)}, u32[]{:S(2)}) async-start(bf16[4,2,65536]{2,1,0:T(2,128)(2,1)} %reshape.628), calls=%async_computation.1 | async-start | bytes 2097152 | tf_op jit(solution)/shard_map/all_to_all | solution.py:194
  212.6 75.7 %copy-start.31 = (f32[1024]{0:T(1024)}, f32[1024]{0:T(1024)S(1)}, u32[]{:S(2)}) copy-start(f32[1024]{0:T(1024)S(1)} %convert_element_type.102) | copy-start | bytes 12292
  236.5 51.8 %copy-start.12 = (f32[512,1024]{1,0:T(8,128)}, f32[512,1024]{1,0:T(8,128)S(1)}, u32[]{:S(2)}) copy-start(f32[512,1024]{1,0:T(8,128)S(1)} %get-tuple-element.449) | copy-start | bytes 6291460
  236.5 51.8 %copy-start.26 = (f32[512]{0:T(512)}, f32[512]{0:T(512)S(1)}, u32[]{:S(2)}) copy-start(f32[512]{0:T(512)S(1)} %broadcast_multiply_fusion.4) | copy-start | bytes 6148
  236.9 51.5 %copy-start.36 = (f32[512]{0:T(512)}, f32[512]{0:T(512)S(1)}, u32[]{:S(2)}) copy-start(f32[512]{0:T(512)S(1)} %add_rsqrt_fusion) | copy-start | bytes 6148
  236.9 27.8 %copy-start.18 = (bf16[1,512,1024]{2,1,0:T(8,128)(2,1)S(1)}, bf16[1,512,1024]{2,1,0:T(8,128)(2,1)}, u32[]{:S(2)}) copy-start(bf16[1,512,1024]{2,1,0:T(8,128)(2,1)} %param.31) | copy-start | bytes 3145732
  278.7 9.6 copy-start.48
  293.4 9.5 copy-start.10
  298.6 18.8 %all-to-all-start.2 = ((bf16[1,512,4,256]{3,1,0,2:T(8,128)(2,1)}), bf16[1,512,4,256]{3,1,0,2:T(8,128)(2,1)}, u32[]{:S(2)}, u32[]{:S(2)}) async-start(bf16[1,512,4,256]{3,1,0,2:T(8,128)(2,1)} %copy.69), calls=%async_computation.2 | async-start | bytes 2097152 | tf_op jit(solution)/shard_map/all_to_all | solution.py:225
  302.8 443.2 %reduce-scatter.10.cloned.1.call-start = ((), (), s32[]{:S(2)}) async-start(), calls=%async_computation.11 | async-start | bytes 4325376 | tf_op jit(solution)/shard_map/reduce_scatter | solution.py:271
  306.1 13.5 %copy-start.5 = (bf16[2048,4,64]{0,2,1:T(8,128)(2,1)S(1)}, bf16[2048,4,64]{0,2,1:T(8,128)(2,1)}, u32[]{:S(2)}) copy-start(bf16[2048,4,64]{0,2,1:T(8,128)(2,1)} %get-tuple-element.718) | copy-start | bytes 3145732
  306.1 13.5 %copy-start.8 = (bf16[2048,4,64]{0,2,1:T(8,128)(2,1)S(1)}, bf16[2048,4,64]{0,2,1:T(8,128)(2,1)}, u32[]{:S(2)}) copy-start(bf16[2048,4,64]{0,2,1:T(8,128)(2,1)} %get-tuple-element.719) | copy-start | bytes 3145732
  306.1 491.7 %reduce-scatter.8.cloned.1.call-start = ((), (), s32[]{:S(2)}) async-start(), calls=%async_computation.10 | async-start | bytes 12976128 | tf_op jit(solution)/shard_map/reduce_scatter | solution.py:270
  344.9 21.7 %copy-start.20 = (bf16[4,512,4,64]{1,3,2,0:T(8,128)(2,1)S(1)}, bf16[4,512,4,64]{1,3,2,0:T(8,128)(2,1)}, u32[]{:S(2)}) copy-start(bf16[4,512,4,64]{1,3,2,0:T(8,128)(2,1)} %get-tuple-element.684) | copy-start | bytes 3145732 | tf_op jit(solution)/shard_map/while/body/eval_jaxpr/while
  360.0 13.4 %copy-start.2 = (f32[4,512,2048]{2,1,0:T(8,128)S(1)}, f32[4,512,2048]{2,1,0:T(8,128)}, u32[]{:S(2)}) copy-start(f32[4,512,2048]{2,1,0:T(8,128)} %get-tuple-element.627) | copy-start | bytes 50331652 | tf_op jit(solution)/shard_map/while/body/eval_jaxpr/while
  373.4 4.1 copy-start.21
  402.9 22.3 %copy-start.20 = (bf16[4,512,4,64]{1,3,2,0:T(8,128)(2,1)S(1)}, bf16[4,512,4,64]{1,3,2,0:T(8,128)(2,1)}, u32[]{:S(2)}) copy-start(bf16[4,512,4,64]{1,3,2,0:T(8,128)(2,1)} %get-tuple-element.684) | copy-start | bytes 3145732 | tf_op jit(solution)/shard_map/while/body/eval_jaxpr/while
  418.0 14.0 %copy-start.2 = (f32[4,512,2048]{2,1,0:T(8,128)S(1)}, f32[4,512,2048]{2,1,0:T(8,128)}, u32[]{:S(2)}) copy-start(f32[4,512,2048]{2,1,0:T(8,128)} %get-tuple-element.627) | copy-start | bytes 50331652 | tf_op jit(solution)/shard_map/while/body/eval_jaxpr/while
  432.0 5.0 copy-start.21
  462.4 22.2 %copy-start.20 = (bf16[4,512,4,64]{1,3,2,0:T(8,128)(2,1)S(1)}, bf16[4,512,4,64]{1,3,2,0:T(8,128)(2,1)}, u32[]{:S(2)}) copy-start(bf16[4,512,4,64]{1,3,2,0:T(8,128)(2,1)} %get-tuple-element.684) | copy-start | bytes 3145732 | tf_op jit(solution)/shard_map/while/body/eval_jaxpr/while
  477.3 14.0 %copy-start.2 = (f32[4,512,2048]{2,1,0:T(8,128)S(1)}, f32[4,512,2048]{2,1,0:T(8,128)}, u32[]{:S(2)}) copy-start(f32[4,512,2048]{2,1,0:T(8,128)} %get-tuple-element.627) | copy-start | bytes 50331652 | tf_op jit(solution)/shard_map/while/body/eval_jaxpr/while
  491.3 5.0 copy-start.21
  521.6 22.2 %copy-start.20 = (bf16[4,512,4,64]{1,3,2,0:T(8,128)(2,1)S(1)}, bf16[4,512,4,64]{1,3,2,0:T(8,128)(2,1)}, u32[]{:S(2)}) copy-start(bf16[4,512,4,64]{1,3,2,0:T(8,128)(2,1)} %get-tuple-element.684) | copy-start | bytes 3145732 | tf_op jit(solution)/shard_map/while/body/eval_jaxpr/while
  536.6 14.0 %copy-start.2 = (f32[4,512,2048]{2,1,0:T(8,128)S(1)}, f32[4,512,2048]{2,1,0:T(8,128)}, u32[]{:S(2)}) copy-start(f32[4,512,2048]{2,1,0:T(8,128)} %get-tuple-element.627) | copy-start | bytes 50331652 | tf_op jit(solution)/shard_map/while/body/eval_jaxpr/while
  550.6 5.0 copy-start.21
  556.0 3.8 copy-start.7
  559.7 2.0 copy-start.17
  624.9 4.8 copy-start.15
  624.9 4.8 copy-start.29
  624.9 4.9 copy-start.34
  624.9 4.9 copy-start.40
  638.4 8.7 copy-start.11
  638.4 310.7 %reduce-scatter.6.cloned.1.call-start = ((), (), s32[]{:S(2)}) async-start(), calls=%async_computation.9 | async-start | bytes 8650752 | tf_op jit(solution)/shard_map/reduce_scatter | solution.py:268
  638.5 8.7 copy-start.16
  647.1 1.8 copy-start.46
  647.1 1.8 copy-start.47
  654.6 1.7 copy-start.37
  654.6 476.3 %reduce-scatter.12.cloned.1.call-start = ((), (), s32[]{:S(2)}) async-start(), calls=%async_computation.12 | async-start | bytes 17301504 | tf_op jit(solution)/shard_map/reduce_scatter | solution.py:273
  667.6 650.7 %reduce-scatter.14.cloned.1.call-start = ((), (), s32[]{:S(2)}) async-start(), calls=%async_computation.13 | async-start | bytes 17301504 | tf_op jit(solution)/shard_map/reduce_scatter | solution.py:275
  680.6 10.9 copy-start.30
  680.6 10.9 copy-start.35
  680.6 10.9 copy-start.41
  680.7 59.1 %copy-start.23 = (bf16[512,1024]{1,0:T(8,128)(2,1)S(1)}, bf16[512,1024]{1,0:T(8,128)(2,1)}, u32[]{:S(2)}) copy-start(bf16[512,1024]{1,0:T(8,128)(2,1)} %copy-done.22) | copy-start | bytes 3145732
  739.8 578.5 %copy-start.1 = (bf16[1024,1024]{1,0:T(8,128)(2,1)S(1)}, bf16[1024,1024]{1,0:T(8,128)(2,1)}, u32[]{:S(2)}) copy-start(bf16[1024,1024]{1,0:T(8,128)(2,1)} %param.25) | copy-start | bytes 6291460
  (11 other events, 13.8 us)
Sparse Core Ops, SparseCore 0:
  306.5 143.4 reduce-scatter.9
  638.5 159.2 reduce-scatter.7
  800.8 148.2 reduce-scatter.5
  951.9 178.8 reduce-scatter.11
  1133.7 184.5 reduce-scatter.13
where the time goes:
time: 1330 us; the launch traced here: 1320 us
  waiting for transfers between devices  634 us (48%)
  matrix products  356 us (27%)
  other arithmetic  121 us (9%)
  blocking collectives  97.8 us (7%)
  local copies, waits for them, and re-layouts  87.9 us (7%)
  between operations  14.5 us (1%)
    reduce_scatter x1, waiting for transfers between devices, body(): lax.psum_scatter(down_grad, ('rows', 'seq'), scatter_dimension=0, tiled=T...  187 us
    reduce_scatter x1, waiting for transfers between devices, body(): lax.psum_scatter(up_grad, ('rows', 'seq'), scatter_dimension=0, tiled=True)  182 us
    reduce_scatter x1, waiting for transfers between devices, body(): lax.psum_scatter(skip_w_grad, ('rows', 'seq'), scatter_dimension=0, tiled...  151 us
    dot_general x8, matrix products, block_scores(): jnp.einsum('qhd,khd->hqk', q_blk, all_keys, preferred_element_type=jnp.fl...  81 us
    convert_element_type x4, other arithmetic, one_block(): score_grad = (soft * (prob_grad - jnp.sum(soft * prob_grad, axis=-1, keep...  60.1 us
    all_to_all x1, blocking collectives, body(): lax.all_to_all(packed_grad, 'seq', split_axis=1, concat_axis=3, tiled=True)  51.9 us
    reduce_scatter x1, waiting for transfers between devices, body(): lax.psum_scatter(qkv_grad, ('rows', 'seq'), scatter_dimension=0, tiled=True)  51.8 us
    unnamed x1, blocking collectives  45.8 us
  transfers between devices with their start and end apart: 8, of which 7 were waited for; matrix products, arithmetic and copies ran while one was open for 25% of the time, Pallas kernels for 0%

commit v1 on v0

--- a/solution.py
+++ b/solution.py
@@ -1,16 +1,28 @@
+import functools
 import math
 
 import jax
 import jax.numpy as jnp
 from jax import lax
+from jax.experimental import pallas as pl
+from jax.experimental.pallas import tpu as pltpu
 from jax.sharding import PartitionSpec as P
 
 D = 1024
 H = 16
 HD = 64
-
+MOST = 682
 
 epsilon = 1e-05
+
+F32 = jnp.float32
+BF16 = jnp.bfloat16
+LOG2E = 1.4426950408889634
+FAR = 1e30
+MESH = pl.DeviceIdType.MESH
+VMEM = pltpu.MemorySpace.VMEM
+SMEM = pltpu.MemorySpace.SMEM
+HBM = pltpu.MemorySpace.HBM
 
 
 def norm_forward(value, gain_vec):
@@ -23,7 +35,7 @@
 
 def norm_backward(upstream, unit, inverse, gain_vec):
     scaled = upstream * gain_vec
-    gain_grad = jnp.sum(upstream * unit, axis=(0, 1))
+    gain_grad = jnp.sum(upstream * unit, axis=tuple(range(upstream.ndim - 1)))
     inner = (
         scaled
         - jnp.mean(scaled, axis=-1, keepdims=True)
@@ -34,6 +46,656 @@
 
 def gelu_exact(value):
     return jax.nn.gelu(value, approximate=False)
+
+
+def mm(equation, left, right):
+    return jnp.einsum(equation, left, right, preferred_element_type=F32)
+
+
+def dot(left, right):
+    return jnp.dot(left, right, preferred_element_type=F32)
+
+
+def set_distances(dist, key_at, query_at, key_code, query_seg):
+    keys, queries = dist.shape
+    rows = lax.broadcasted_iota(jnp.int32, (keys, queries), 0) + key_at
+    cols = lax.broadcasted_iota(jnp.int32, (keys, queries), 1) + query_at
+    apart = jnp.abs(rows - cols)
+    allowed = (key_code == query_seg) | (apart == 0)
+    dist[...] = jnp.where(allowed, apart.astype(F32), FAR)
+
+
+def wide(code, queries):
+    return jnp.concatenate([code] * (queries // 128), axis=1) if queries > 128 else code
+
+
+def blocks_meet(kspan, qspan, j, i):
+    return (kspan[0, j] <= qspan[1, i]) & (kspan[1, j] >= qspan[0, i])
+
+
+def attend_kernel(
+    bq, bk, heads, kspan, qspan, slopes, qt, kv, vt, kcode, qseg, out, lse, dist, acc, top, total
+):
+    width = heads * HD
+    c1 = LOG2E / math.sqrt(HD)
+    blank = jnp.zeros((HD, bq), BF16)
+
+    def q_block(i, _):
+        qs = pl.multiple_of(i * bq, bq)
+        acc[...] = jnp.zeros_like(acc)
+        total[...] = jnp.zeros_like(total)
+        top[...] = jnp.full_like(top, -3e38)
+
+        def k_block(j, _):
+            @pl.when(blocks_meet(kspan, qspan, j, i))
+            def _():
+                ks = pl.multiple_of(j * bk, bk)
+                set_distances(
+                    dist,
+                    kspan[2, j],
+                    qspan[2, i],
+                    wide(kcode[pl.ds(ks, bk), :], bq),
+                    qseg[0:1, pl.ds(qs, bq)],
+                )
+                for h in range(heads):
+                    mine = qt[pl.ds(HD * h, HD), pl.ds(qs, bq)]
+                    pair = [mine, blank] if h % 2 == 0 else [blank, mine]
+                    score = dot(
+                        kv[pl.ds(ks, bk), pl.ds(128 * (h // 2), 128)],
+                        jnp.concatenate(pair, axis=0),
+                    )
+                    score = score * c1 - dist[...] * slopes[h]
+                    was = top[h : h + 1, :]
+                    now = jnp.maximum(was, jnp.max(score, axis=0, keepdims=True))
+                    prob = jnp.exp2(score - now)
+                    fade = jnp.exp2(was - now)
+                    total[h : h + 1, :] = total[h : h + 1, :] * fade + jnp.sum(
+                        prob, axis=0, keepdims=True
+                    )
+                    top[h : h + 1, :] = now
+                    acc[pl.ds(HD * h, HD), :] = acc[pl.ds(HD * h, HD), :] * fade + dot(
+                        vt[pl.ds(HD * h, HD), pl.ds(ks, bk)], prob.astype(BF16)
+                    )
+
+            return 0
+
+        lax.fori_loop(0, kv.shape[0] // bk, k_block, 0)
+        for h in range(heads):
+            acc[pl.ds(HD * h, HD), :] = acc[pl.ds(HD * h, HD), :] * (1.0 / total[h : h + 1, :])
+        lse[:, pl.ds(qs, bq)] = top[...] + jnp.log2(total[...])
+        out[pl.ds(qs, bq), :] = acc[...].T.astype(BF16)
+        return 0
+
+    lax.fori_loop(0, qt.shape[1] // bq, q_block, 0)
+
+
+def attend(kspan, qspan, slopes, qt, kv, vt, kcode, qseg, bq, bk, heads):
+    frames = qt.shape[1]
+    vm, sm = pl.BlockSpec(memory_space=VMEM), pl.BlockSpec(memory_space=SMEM)
+    return pl.pallas_call(
+        functools.partial(attend_kernel, bq, bk, heads),
+        out_shape=(
+            jax.ShapeDtypeStruct((frames, heads * HD), BF16),
+            jax.ShapeDtypeStruct((heads, frames), F32),
+        ),
+        in_specs=[sm] * 3 + [vm] * 5,
+        out_specs=(vm, vm),
+        scratch_shapes=[
+            pltpu.VMEM((bk, bq), F32),
+            pltpu.VMEM((heads * HD, bq), F32),
+            pltpu.VMEM((heads, bq), F32),
+            pltpu.VMEM((heads, bq), F32),
+        ],
+        name="attend",
+        cost_estimate=pl.CostEstimate(
+            flops=8_000_000_000, bytes_accessed=8_000_000, transcendentals=4_000_000
+        ),
+        compiler_params=pltpu.CompilerParams(vmem_limit_bytes=32 << 20),
+    )(kspan, qspan, slopes, qt, kv, vt, kcode, qseg)
+
+
+def attend_back_kernel(
+    bq,
+    bk,
+    heads,
+    kspan,
+    qspan,
+    slopes,
+    q,
+    qt,
+    kv,
+    kt,
+    grad,
+    gradt,
+    lse,
+    delta,
+    kcode,
+    qseg,
+    dq,
+    dkv,
+    dist,
+    dqt,
+    sums,
+):
+    width = heads * HD
+    c1 = LOG2E / math.sqrt(HD)
+    scale = 1.0 / math.sqrt(HD)
+    blank = jnp.zeros((HD, bq), BF16)
+    lane = lax.broadcasted_iota(jnp.int32, (bq, 128), 1)
+    sums[...] = jnp.zeros_like(sums)
+
+    def q_block(i, _):
+        qs = pl.multiple_of(i * bq, bq)
+        dqt[...] = jnp.zeros_like(dqt)
+
+        def k_block(j, _):
+            @pl.when(blocks_meet(kspan, qspan, j, i))
+            def _():
+                ks = pl.multiple_of(j * bk, bk)
+                set_distances(
+                    dist,
+                    kspan[2, j],
+                    qspan[2, i],
+                    wide(kcode[pl.ds(ks, bk), :], bq),
+                    qseg[0:1, pl.ds(qs, bq)],
+                )
+                for pair in range(heads // 2):
+                    at = pl.ds(128 * pair, 128)
+                    keys = kv[pl.ds(ks, bk), at]
+                    values = kv[pl.ds(ks, bk), pl.ds(width + 128 * pair, 128)]
+                    grads = grad[pl.ds(qs, bq), at]
+                    queries = q[pl.ds(qs, bq), at]
+                    dk, dv = None, None
+                    for e in range(2):
+                        h = 2 * pair + e
+                        keep = (lane < HD) if e == 0 else (lane >= HD)
+
+                        def padded(ref):
+                            mine = ref[pl.ds(HD * h, HD), pl.ds(qs, bq)]
+                            return jnp.concatenate(
+                                [mine, blank] if e == 0 else [blank, mine], axis=0
+                            )
+
+                        score = dot(keys, padded(qt))
+                        prob = jnp.exp2(
+                            score * c1
+                            - dist[...] * slopes[h]
+                            - lse[h : h + 1, pl.ds(qs, bq)]
+                        )
+                        prob_grad = dot(values, padded(gradt))
+                        score_grad = (
+                            prob * (prob_grad - delta[h : h + 1, pl.ds(qs, bq)])
+                        ).astype(BF16)
+                        dvh = dot(prob.astype(BF16), jnp.where(keep, grads, jnp.zeros_like(grads)))
+                        dkh = dot(score_grad, jnp.where(keep, queries, jnp.zeros_like(queries)))
+                        dv = dvh if dv is None else dv + dvh
+                        dk = dkh if dk is None else dk + dkh
+                        dqt[pl.ds(HD * h, HD), :] += dot(
+                            kt[pl.ds(HD * h, HD), pl.ds(ks, bk)], score_grad
+                        )
+                    sums[pl.ds(ks, bk), at] += dk
+                    sums[pl.ds(ks, bk), pl.ds(width + 128 * pair, 128)] += dv
+
+            return 0
+
+        lax.fori_loop(0, kv.shape[0] // bk, k_block, 0)
+        dq[pl.ds(qs, bq), :] = (dqt[...] * scale).T.astype(BF16)
+        return 0
+
+    lax.fori_loop(0, q.shape[0] // bq, q_block, 0)
+    dkv[:, :width] = (sums[:, :width] * scale).astype(BF16)
+    dkv[:, width:] = sums[:, width:].astype(BF16)
+
+
+def attend_back(
+    kspan, qspan, slopes, q, qt, kv, kt, grad, gradt, lse, delta, kcode, qseg, bq, bk, heads
+):
+    vm, sm = pl.BlockSpec(memory_space=VMEM), pl.BlockSpec(memory_space=SMEM)
+    return pl.pallas_call(
+        functools.partial(attend_back_kernel, bq, bk, heads),
+        out_shape=(
+            jax.ShapeDtypeStruct(q.shape, BF16),
+            jax.ShapeDtypeStruct(kv.shape, BF16),
+        ),
+        in_specs=[sm] * 3 + [vm] * 10,
+        out_specs=(vm, vm),
+        scratch_shapes=[
+            pltpu.VMEM((bk, bq), F32),
+            pltpu.VMEM((heads * HD, bq), F32),
+            pltpu.VMEM(kv.shape, F32),
+        ],
+        name="attend_back",
+        cost_estimate=pl.CostEstimate(
+            flops=20_000_000_000, bytes_accessed=16_000_000, transcendentals=4_000_000
+        ),
+        compiler_params=pltpu.CompilerParams(vmem_limit_bytes=48 << 20),
+    )(kspan, qspan, slopes, q, qt, kv, kt, grad, gradt, lse, delta, kcode, qseg)
+
+
+ROWS, COLS = 32, 1024
+
+
+def share_kernel(
+    plan, down, up, gq, gkv, wo, skip, vec, *refs
+):
+    n_units, n_sums = len(plan), sum(u["core"] == "sum" for u in plan)
+    o_down, o_up, o_qkv, o_wo, o_skip, o_vec = refs[:6]
+    own, r0, r1, r2, r3, ownv, r0v, r1v, r2v, r3v, loads, sends, recvs = refs[6:]
+    sources = {"down": down, "up": up, "gq": gq, "gkv": gkv, "wo": wo, "skip": skip}
+    results = {"down": o_down, "up": o_up, "qkv": o_qkv, "wo": o_wo, "skip": o_skip}
+    row, col = lax.axis_index("rows"), lax.axis_index("seq")
+    z, x, y, c = row // 2, row % 2, col // 2, col % 2
+
+    def device(pz, px, py, pc):
+        return (pz * 2 + px, py * 2 + pc)
+
+    over_core = device(z, x, y, 1 - c)
+    over_y = device(z, x, 1 - y, c)
+    over_x = device(z, 1 - x, y, c)
+    z_at = [(z + d) % 4 for d in range(4)]
+    over_z = [device(p, x, y, c) for p in z_at]
+    barrier = pltpu.get_barrier_semaphore()
+    peers = [over_core, over_y, over_x, over_z[1], over_z[2], over_z[3]]
+    for peer in peers:
+        pl.semaphore_signal(barrier, inc=1, device_id=peer, device_id_type=MESH)
+    pl.semaphore_wait(barrier, len(peers))
+
+    def remote(src, dst, sem, peer):
+        copy = pltpu.make_async_remote_copy(
+            src, dst, sends.at[sem], recvs.at[sem], device_id=peer, device_id_type=MESH
+        )
+        copy.start()
+        return copy
+
+    started = []
+    core_in, local_in = {}, {}
+    for k, unit in enumerate(plan):
+        src = sources[unit["src"]]
+        r, q = pl.ds(unit["row"], ROWS), pl.ds(unit["col"], unit["width"])
+        if unit["core"] == "sum":
+            dst = own.at[k]
+            there = r0.at[unit["slot"]]
+        else:
+            part = pl.ds(pl.multiple_of(c * unit["width"], unit["width"]), unit["width"])
+            dst = own.at[k, :, :, :, :, part]
+            there = dst
+        core_in[k] = remote(src.at[:, :, :, 1 - c, r, q], there, 6 * k, over_core)
+        copy = pltpu.make_async_copy(src.at[:, :, :, c, r, q], dst, loads.at[k])
+        copy.start()
+        local_in[k] = copy
+    k = n_units
+    core_in[k] = remote(vec.at[:, :, :, 1 - c], r0v, 6 * k, over_core)
+    local_in[k] = pltpu.make_async_copy(vec.at[:, :, :, c], ownv, loads.at[k])
+    local_in[k].start()
+
+    first_in, second_in, third_in = {}, {}, {}
+
+    def mine(k):
+        return ownv if k == n_units else own.at[k]
+
+    def buffers(k):
+        if k == n_units:
+            return r1v, r2v, r3v
+        return r1.at[k], r2.at[k], r3.at[k]
+
+    def add_core(k):
+        local_in[k].wait()
+        core_in[k].wait_recv()
+        a = mine(k)
+        if k < n_units and plan[k]["core"] != "sum":
+            return
+        b = r0v if k == n_units else r0.at[plan[k]["slot"]]
+
+        def step(i, _):
+            for j in range(2):
+                for m in range(2):
+                    a[i, j, m] = a[i, j, m] + b[i, j, m]
+            return 0
+
+        lax.fori_loop(0, 4, step, 0)
+
+    def send_first(k):
+        a, to = mine(k), buffers(k)[0]
+        if k % 2 == 0:
+            first_in[k] = remote(a.at[:, :, 1 - y], to, 6 * k + 1, over_y)
+        else:
+            first_in[k] = remote(a.at[:, 1 - x], to, 6 * k + 1, over_x)
+
+    def add_first(k):
+        first_in[k].wait_recv()
+        a, b = mine(k), buffers(k)[0]
+
+        def step(i, _):
+            for j in range(2):
+                if k % 2 == 0:
+                    a[i, j, y] = a[i, j, y] + b[i, j]
+                else:
+                    a[i, x, j] = a[i, x, j] + b[i, j]
+            return 0
+
+        lax.fori_loop(0, 4, step, 0)
+
+    def send_second(k):
+        a, to = mine(k), buffers(k)[1]
+        if k % 2 == 0:
+            second_in[k] = remote(a.at[:, 1 - x, y], to, 6 * k + 2, over_x)
+        else:
+            second_in[k] = remote(a.at[:, x, 1 - y], to, 6 * k + 2, over_y)
+
+    def add_second(k):
+        second_in[k].wait_recv()
+        a, b = mine(k), buffers(k)[1]
+
+        def step(i, _):
+            a[i, x, y] = a[i, x, y] + b[i]
+            return 0
+
+        lax.fori_loop(0, 4, step, 0)
+
+    def send_third(k):
+        a, to = mine(k), buffers(k)[2]
+        third_in[k] = [
+            remote(a.at[z_at[d], x, y], to.at[d - 1], 6 * k + 2 + d, over_z[d])
+            for d in (1, 2, 3)
+        ]
+
+    def finish(k):
+        for copy in third_in[k]:
+            copy.wait_recv()
+        a, b = mine(k), buffers(k)[2]
+        value = a[z, x, y].astype(F32)
+        for d in range(3):
+            value = value + b[d].astype(F32)
+        if k == n_units:
+            o_vec[...] = value
+        else:
+            unit = plan[k]
+            results[unit["out"]][pl.ds(unit["row"], ROWS), pl.ds(unit["out_col"], COLS)] = value
+
+    groups = [[k for k in (p, p + 1) if k < n_units] for p in range(0, n_units, 2)]
+    groups[0] = groups[0] + [n_units]
+    n = len(groups)
+    for t in range(n + 3):
+        if t < n:
+            for k in groups[t]:
+                add_core(k)
+                send_first(k)
+        if 0 <= t - 1 < n:
+            for k in groups[t - 1]:
+                add_first(k)
+                send_second(k)
+        if 0 <= t - 2 < n:
+            for k in groups[t - 2]:
+                add_second(k)
+                send_third(k)
+        if 0 <= t - 3 < n:
+            for k in groups[t - 3]:
+                finish(k)
+    for k in range(n_units + 1):
+        for copy in [core_in[k], first_in[k], second_in[k], *third_in[k]]:
+            copy.wait_send()
+
+
+def share_plan():
+    def one(src, out, row, col, out_col, width=COLS, core="sum"):
+        return dict(src=src, out=out, row=row, col=col, out_col=out_col, width=width, core=core)
+
+    down = [one("down", "down", ROWS * i, 0, 0) for i in range(4)]
+    up = [one("up", "up", 0, COLS * i, COLS * i) for i in range(4)]
+    qkv = [
+        one("gq", "qkv", 0, 0, 0, COLS // 2, "join"),
+        one("gkv", "qkv", 0, 0, COLS, COLS // 2, "join"),
+        one("gkv", "qkv", 0, COLS // 2, 2 * COLS, COLS // 2, "join"),
+    ]
+    skip = [one("skip", "skip", ROWS * i, 0, 0) for i in range(2)]
+    wo = [one("wo", "wo", 0, 0, 0)]
+    plan = [u for pair in zip(down, up) for u in pair]
+    plan += [qkv[0], skip[0], qkv[1], skip[1], qkv[2], wo[0]]
+    slot = 0
+    for unit in plan:
+        if unit["core"] == "sum":
+            unit["slot"] = slot
+            slot += 1
+    return plan, slot
+
+
+def share(down, up, gq, gkv, wo, skip, vec):
+    plan, slots = share_plan()
+    n = len(plan)
+
+    def cut(value):
+        return value.reshape(4, 2, 2, 2, value.shape[0] // 32, value.shape[1])
+
+    hbm, vm = pl.BlockSpec(memory_space=HBM), pl.BlockSpec(memory_space=VMEM)
+    unit = (ROWS, COLS)
+    small = (8, 128)
+    args = [cut(v) for v in (down, up, gq, gkv, wo, skip)] + [vec.reshape(4, 2, 2, 2, *small)]
+    outs = [(128, 1024), (32, 4096), (32, 3072), (32, 1024), (64, 1024), small]
+    return pl.pallas_call(
+        functools.partial(share_kernel, plan),
+        out_shape=[jax.ShapeDtypeStruct(s, F32) for s in outs],
+        in_specs=[hbm] * 7,
+        out_specs=[vm] * 6,
+        scratch_shapes=[
+            pltpu.VMEM((n, 4, 2, 2, *unit), BF16),
+            pltpu.VMEM((slots, 4, 2, 2, *unit), BF16),
+            pltpu.VMEM((n, 4, 2, *unit), BF16),
+            pltpu.VMEM((n, 4, *unit), BF16),
+            pltpu.VMEM((n, 3, *unit), BF16),
+            pltpu.VMEM((4, 2, 2, *small), F32),
+            pltpu.VMEM((4, 2, 2, *small), F32),
+            pltpu.VMEM((4, 2, *small), F32),
+            pltpu.VMEM((4, *small), F32),
+            pltpu.VMEM((3, *small), F32),
+            pltpu.SemaphoreType.DMA((n + 1,)),
+            pltpu.SemaphoreType.DMA((6 * (n + 1),)),
+            pltpu.SemaphoreType.DMA((6 * (n + 1),)),
+        ],
+        name="share",
+        cost_estimate=pl.CostEstimate(flops=30_000_000, bytes_accessed=60_000_000, transcendentals=0),
+        compiler_params=pltpu.CompilerParams(
+            collective_id=0, has_side_effects=True, vmem_limit_bytes=52 << 20
+        ),
+    )(*args)
+
+
+CHIP = 1024
+HALO = 768
+
+
+def swap_core(value):
+    return lax.ppermute(value, "seq", [(i, i ^ 1) for i in range(4)])
+
+
+def swap_chip(value):
+    return lax.ppermute(value, "seq", [(i, i ^ 2) for i in range(4)])
+
+
+def body_chips(
+    inputs,
+    skip_feats,
+    seg_ids,
+    frame_valid,
+    w_skip,
+    gain_one,
+    w_qkv,
+    w_out,
+    gain_two,
+    w_up,
+    b_up,
+    w_down,
+    b_down,
+    cotangent,
+):
+    here = lax.axis_index("seq")
+    y, c = here // 2, here % 2
+    frames = inputs.shape[1]
+    heads = H // 2
+    width = heads * HD
+    first, second_in, cot = inputs[0], skip_feats[0], cotangent[0]
+    gain_first = gain_one.astype(F32)
+    gain_second = gain_two.astype(F32)
+
+    halo_at = jnp.where(y == 0, CHIP, CHIP - HALO)
+    own_at, other_at = here * frames, (here ^ 1) * frames
+    seg_row = seg_ids[0]
+    code_row = jnp.where(frame_valid[0] == 1, seg_row, -1)
+
+    def seen(row):
+        return jnp.concatenate(
+            [
+                lax.dynamic_slice(row, (own_at,), (frames,)),
+                lax.dynamic_slice(row, (other_at,), (frames,)),
+                lax.dynamic_slice(row, (halo_at,), (HALO,)),
+            ]
+        )
+
+    seg_seen = seen(seg_row)
+    kcode = jnp.broadcast_to(seen(code_row)[:, None], (CHIP + HALO, 128))
+    qseg = jnp.broadcast_to(seg_seen[None, :CHIP], (8, CHIP))
+
+    def spans(count, block):
+        at = jnp.arange(0, count, block)
+        base = jnp.where(at < frames, own_at, jnp.where(at < CHIP, other_at - frames, halo_at - CHIP))
+        seg = seg_seen[:count].reshape(-1, block)
+        return jnp.stack([seg[:, 0], seg[:, -1], base + at]).astype(jnp.int32)
+
+    slopes = LOG2E * jnp.exp2(-8.0 * (c * heads + jnp.arange(heads) + 1).astype(F32) / H)
+
+    w_heads = lax.dynamic_index_in_dim(w_qkv.reshape(D, 3, 2, width), c, 2, keepdims=False)
+    w_q, w_kv = w_heads[:, 0], w_heads[:, 1:].reshape(D, 2 * width)
+
+    joined = jnp.concatenate([first, second_in], axis=-1)
+    stem_out = mm("fc,cd->fd", joined, w_skip)
+    unit_one, inverse_one, normed = norm_forward(stem_out, gain_first)
+    normed = normed.astype(BF16)
+    normed_other = swap_core(normed)
+    around = jnp.concatenate([normed, normed_other, normed], axis=0)
+    half = HALO // 2
+    part_at = c * frames + jnp.where(y == 0, CHIP - HALO, 0) + half * c
+    halo_part = swap_chip(lax.dynamic_slice(around, (part_at, 0), (half, D)))
+    halo_rest = swap_core(halo_part)
+    halo_parts = jnp.concatenate([halo_part, halo_rest, halo_part], axis=0)
+    halo = lax.dynamic_slice(halo_parts, (c * half, 0), (HALO, D))
+    normed_seen = jnp.concatenate([normed, normed_other, halo], axis=0)
+    q = mm("fd,de->fe", normed_seen[:CHIP], w_q).astype(BF16)
+    kv = mm("fd,de->fe", normed_seen, w_kv).astype(BF16)
+
+    attended, lse = attend(
+        spans(CHIP + HALO, 128),
+        spans(CHIP, 128),
+        slopes,
+        q.T,
+        kv,
+        kv[:, width:].T,
+        kcode,
+        qseg,
+        128,
+        128,
+        heads,
+    )
+    attended_other = swap_core(attended[frames:])
+    pair = jnp.concatenate([attended[:frames], attended_other, attended[:frames]], axis=1)
+    mixed_out = lax.dynamic_slice(pair, (0, c * width), (frames, D))
+    middle = stem_out + mm("fd,de->fe", mixed_out, w_out)
+    unit_two, inverse_two, second = norm_forward(middle, gain_second)
+    second = second.astype(BF16)
+    hidden = mm("fd,dk->fk", second, w_up) + b_up.astype(F32)
+    active_full, gelu_back = jax.vjp(gelu_exact, hidden)
+    active = active_full.astype(BF16)
+    result = middle + mm("fk,kd->fd", active, w_down) + b_down.astype(F32)
+    output = result.astype(BF16)
+    cot_full = cot.astype(F32)
+    down_grad = mm("fk,fd->kd", active, cot).astype(BF16)
+    bias_down_grad = jnp.sum(cot_full, axis=0)
+    active_grad = mm("fd,kd->fk", cot, w_down)
+    hidden_grad = gelu_back(active_grad)[0].astype(BF16)
+    up_grad = mm("fd,fk->dk", second, hidden_grad).astype(BF16)
+    bias_up_grad = jnp.sum(hidden_grad.astype(F32), axis=0)
+    second_grad = mm("fk,dk->fd", hidden_grad, w_up)
+    middle_part, gain_two_grad = norm_backward(second_grad, unit_two, inverse_two, gain_second)
+    middle_grad = cot_full + middle_part
+    middle_low = middle_grad.astype(BF16)
+    out_grad = mm("fd,fe->de", mixed_out, middle_low).astype(BF16)
+    mixed_grad = mm("fe,de->fd", middle_low, w_out).astype(BF16)
+    mixed_halves = mixed_grad.reshape(frames, 2, width)
+    grad_own = lax.dynamic_index_in_dim(mixed_halves, c, 1, keepdims=False)
+    grad_other = swap_core(lax.dynamic_index_in_dim(mixed_halves, 1 - c, 1, keepdims=False))
+    grad_heads = jnp.concatenate([grad_own, grad_other], axis=0)
+    delta = jnp.sum(
+        (attended.astype(F32) * grad_heads.astype(F32)).reshape(CHIP, heads, HD), axis=-1
+    ).T
+    dq, dkv = attend_back(
+        spans(CHIP + HALO, 256),
+        spans(CHIP, 512),
+        slopes,
+        q,
+        q.T,
+        kv,
+        kv[:, :width].T,
+        grad_heads,
+        grad_heads.T,
+        lse,
+        delta,
+        kcode,
+        qseg,
+        512,
+        256,
+        heads,
+    )
+    halo_grad = mm("fe,de->fd", dkv[CHIP:], w_kv).astype(BF16)
+    halo_mine = lax.dynamic_slice(halo_grad, (c * half, 0), (half, D))
+    halo_theirs = lax.dynamic_slice(halo_grad, ((1 - c) * half, 0), (half, D))
+    halo_sum = (halo_mine.astype(F32) + swap_core(halo_theirs).astype(F32)).astype(BF16)
+    back_part = swap_chip(halo_sum)
+    back_rest = swap_core(back_part)
+    back = lax.dynamic_slice(
+        jnp.concatenate([back_part, back_rest, back_part], axis=0), (c * half, 0), (HALO, D)
+    )
+    edge = CHIP - HALO
+    back = lax.dynamic_slice(
+        jnp.pad(back, ((edge, edge), (0, 0))), (c * frames + y * edge, 0), (frames, D)
+    )
+    qkv_grad_q = mm("fd,fe->de", normed_seen[:CHIP], dq).astype(BF16)
+    qkv_grad_kv = mm("fd,fe->de", normed_seen, dkv).astype(BF16)
+    chip_grad = mm("fe,de->fd", dq, w_q) + mm("fe,de->fd", dkv[:CHIP], w_kv)
+    from_core = swap_core(chip_grad[frames:].astype(BF16))
+    normed_grad = chip_grad[:frames] + from_core.astype(F32) + back.astype(F32)
+    stem_part, gain_one_grad = norm_backward(normed_grad, unit_one, inverse_one, gain_first)
+    stem_low = (middle_grad + stem_part).astype(BF16)
+    skip_w_grad = mm("fc,fd->cd", joined, stem_low).astype(BF16)
+    joined_grad = mm("fd,cd->fc", stem_low, w_skip)
+    input_grad = joined_grad[:, :D].astype(BF16)
+    skip_grad = joined_grad[:, D:].astype(BF16)
+
+    vec = jnp.concatenate(
+        [
+            bias_up_grad.reshape(32, 128),
+            gain_one_grad.reshape(32, 32),
+            gain_two_grad.reshape(32, 32),
+            bias_down_grad.reshape(32, 32),
+            jnp.zeros((32, 1024 - 224), F32),
+        ],
+        axis=1,
+    )
+    down_share, up_share, qkv_share, out_share, skip_share, vec_share = share(
+        down_grad, up_grad, qkv_grad_q, qkv_grad_kv, out_grad, skip_w_grad, vec
+    )
+    small = vec_share[1]
+    return (
+        output[None],
+        input_grad[None],
+        skip_grad[None],
+        skip_share,
+        small[0:32],
+        qkv_share,
+        out_share,
+        small[32:64],
+        up_share,
+        vec_share[0],
+        down_share,
+        small[64:96],
+    )
 
 
 def block_scores(q_blk, pos_blk, seg_blk, all_keys, seg_row, valid_row, slopes, score_scale):
@@ -292,8 +954,9 @@
 
 
 def solution(mesh):
+    fits = (mesh.shape["rows"], mesh.shape["seq"]) == (8, 4)
     return jax.shard_map(
-        body,
+        body_chips if fits else body,
         mesh=mesh,
         in_specs=(
             P("rows", "seq", None),

time: 1330 us -> 452 us (0.34)
  waiting for transfers between devices: 634 us -> 18.8 us
  matrix products: 356 us -> 124 us
  Pallas kernels: 0 us -> 198 us
  blocking collectives: 97.8 us -> 0 us
  other arithmetic: 121 us -> 23.3 us
  local copies, waits for them, and re-layouts: 87.9 us -> 61.8 us
    reduce_scatter x5 -> x0, waiting for transfers between devices: 572 us -> none  [the longest x1 187 us: body(): lax.psum_scatter(down_grad, ('rows', 'seq'), scatter_dimension=0, tiled=T...]
    dot_general x43 -> x19, matrix products: 356 us -> 124 us  [mm(): return jnp.einsum(equation, left, right, preferred_element_type=F32)]
    pallas_call x0 -> x3, Pallas kernels: none -> 198 us  [the longest x1 151 us: share(): pl.pallas_call(functools.partial(share_kernel, plan), out_shape=[jax.Shap...]
    all_to_all x3 -> x0, waiting for transfers between devices: 61.9 us -> none  [the longest x1 36.4 us: body(): lax.all_to_all(packed, 'seq', split_axis=3, concat_axis=1, tiled=True)]
    convert_element_type x16 -> x7, other arithmetic: 66.1 us -> 4.31 us  [the longest x1 3.66 us: body_chips(): stem_low = (middle_grad + stem_part).astype(BF16)]
    all_to_all x1 -> x0, blocking collectives: 51.9 us -> none  [body(): lax.all_to_all(packed_grad, 'seq', split_axis=1, concat_axis=3, tiled=True)]
    unnamed x1 -> x0, blocking collectives: 45.8 us -> none
    reshape x6, local copies, waits for them, and re-layouts: 21.9 us -> 0.77 us  [the longest x1 0.54 us: body_chips(): mixed_halves = mixed_grad.reshape(frames, 2, width)]
  transfers between devices with their start and end apart: 8 -> 9, of which waited for: 7 -> 3; matrix products, arithmetic and copies ran while one was open for 25% -> 18% of each run, Pallas kernels for 0% -> 0%
where the time goes in v1:
time: 452 us; the launch traced here: 445 us
  Pallas kernels  198 us (44%)
  matrix products  124 us (27%)
  local copies, waits for them, and re-layouts  61.8 us (14%)
  other arithmetic  23.3 us (5%)
  waiting for transfers between devices  18.8 us (4%)
  starting transfers between devices  17.4 us (4%)
    pallas_call x1, Pallas kernels, share(): pl.pallas_call(functools.partial(share_kernel, plan), out_shape=[jax.Shap...  151 us
    dot_general x19, matrix products, mm(): return jnp.einsum(equation, left, right, preferred_element_type=F32)  124 us
    pallas_call x1, Pallas kernels, attend_back(): pl.pallas_call(functools.partial(attend_back_kernel, bq, bk, heads), out_...  29.9 us
    unnamed x105, local copies, waits for them, and re-layouts  25.6 us
    pallas_call x1, Pallas kernels, attend(): pl.pallas_call(functools.partial(attend_kernel, bq, bk, heads), out_shape...  17.4 us
    ppermute x2, waiting for transfers between devices, swap_chip(): return lax.ppermute(value, 'seq', [(i, i ^ 2) for i in range(4)])  16.4 us
    ppermute x2, starting transfers between devices, swap_chip(): return lax.ppermute(value, 'seq', [(i, i ^ 2) for i in range(4)])  15.8 us
  transfers between devices with their start and end apart: 9, of which 3 were waited for; matrix products, arithmetic and copies ran while one was open for 18% of the time, Pallas kernels for 0%

profile of v1, /device:TPU:0, one launch (start us, length us, event | category | flops | bytes accessed | tf_op | source)
XLA Modules:
  0.0 444.7 jit_solution(7976721598011890816)
XLA Ops:
  0.7 5.4 %fusion.45 = (f32[512]{0:T(512)S(1)}, f32[512,1024]{1,0:T(8,128)S(1)}) fusion(bf16[2048,1024]{1,0:T(8,128)(2,1)} %param.18, bf16[512,1024]{1,0:T(8,128)(2,1)} %bitcast.135, bf16[512,1024]{1,0:T(8,128)(2,1)} %bitcast.137), kind=kOutput, calls=%fused_computation.157 | convolution fusion | flops 2152201728 | bytes 8390656 | tf_op jit(solution)/shard_map/fc,cd->fd/dot_general | solution.py:52
  6.5 0.9 copy-done.10
  8.5 2.3 collective-permute-done
  10.9 3.0 fusion.24
  13.9 2.0 collective-permute-start.1
  15.8 9.2 %copy.48 = bf16[1024,3072]{0,1:T(8,128)(2,1)} copy(bf16[1024,3072]{1,0:T(8,128)(2,1)} %param.20) | data formatting | bytes 12582912 | tf_op args[6]
  25.3 3.9 constant_dynamic-slice_fusion.4
  29.2 5.1 %collective-permute-done.1 = bf16[384,1024]{1,0:T(8,128)(2,1)} collective-permute-done((bf16[384,1024]{1,0:T(8,128)(2,1)}, bf16[384,1024]{1,0:T(8,128)(2,1)}, u32[]{:S(2)}, u32[]{:S(2)}) %collective-permute-start.1) | collective-permute-done | bytes 786464 | tf_op jit(solution)/shard_map/ppermute | solution.py:511
  34.4 4.7 %copy.49 = bf16[1024,3,1,512]{3,0,2,1:T(8,128)(2,1)} copy(bf16[1024,3,1,512]{0,3,2,1:T(8,128)(2,1)} %constant_dynamic-slice_fusion.4) | data formatting | bytes 6291456 | tf_op jit(solution)/shard_map/jit(dynamic_index_in_dim)/dynamic_slice | solution.py:565
  39.1 3.1 slice.126
  42.2 4.0 copy.51
  46.5 3.8 convolution_convert_fusion.10
  50.3 3.0 fusion.12
  53.4 5.8 %convolution_convert_fusion.3 = bf16[1792,1024]{0,1:T(8,128)(2,1)S(1)} fusion(bf16[1024,1024]{0,1:T(8,128)(2,1)S(1)} %bitcast.111, bf16[768,1024]{1,0:T(8,128)(2,1)S(1)} %fusion.12, bf16[512,1024]{1,0:T(8,128)(2,1)} %collective-permute-done, bf16[512,1024]{1,0:T(8,128)(2,1)S(1)} %multiply_convert_fusion.2), kind=kOutput, calls=%fused_computation.21 | convolution fusion | flops 3770941440 | bytes 9437184 | tf_op jit(solution)/shard_map/fd,de->fe/dot_general | solution.py:52
  59.2 1.8 copy-done.12
  61.0 2.1 slice_bitcast_fusion
  63.1 5.9 %copy.53.kv = bf16[1792,1024]{1,0:T(8,128)(2,1)} copy(bf16[1792,1024]{0,1:T(8,128)(2,1)} %copy-done.12) | data formatting | bytes 7340032 | tf_op jit(solution)/shard_map/convert_element_type | solution.py:582
  69.3 2.4 copy-done.2
  71.6 1.5 copy-done.3
  73.1 1.2 copy-done.4
  74.3 17.4 %attend.1 = (bf16[1024,512]{1,0:T(8,128)(2,1)S(1)}, f32[8,1024]{1,0:T(8,128)S(1)}) custom-call(s32[3,14]{1,0:T(4,128)S(1)} %pad_add_fusion.4.kspan, s32[3,8]{1,0:T(4,128)S(1)} %pad_add_fusion.5.qspan, f32[8]{0:T(128)S(1)} %exponential_multiply_fusion.slopes, bf16[512,1024]{1,0:T(8,128)(2,1)S(1)} %bitcast.97, bf16[1792,1024]{1,0:T(8,128)(2,1)S(1)} %copy-done.2, ...), custom_call_target="tpu_custom_call" | custom-call | flops 8000000000 | bytes 8000000 | tf_op jit(solution)/shard_map/attend/pallas_call | solution.py:135
  91.7 1.0 fusion.44
  93.6 2.3 copy.57.q
  95.8 1.3 copy.56
  97.1 1.9 fusion.17
  99.1 3.3 fusion.46
  102.9 25.6 %multiply_convert_fusion = (bf16[512,4096]{1,0:T(8,128)(2,1)}, f32[512,4096]{1,0:T(8,128)}, f32[512,4096]{1,0:T(8,128)}) fusion(f32[4096]{0:T(1024)S(1)} %convert_element_type.108, bf16[1024,4096]{1,0:T(8,128)(2,1)S(1)} %bitcast.134, f32[512,1024]{1,0:T(8,128)S(1)} %get-tuple-element.73, f32[1024]{0:T(1024)S(1)} %convert_element_type.106, ...), kind=kOutput, calls=%fused_computation.4 | convolution fusion | flops 4435476480 | bytes 31481856 | tf_op jit(solution)/shard_map/fd,dk->fk/dot_general | solution.py:52
  128.5 14.7 %convert_reduce_fusion = (f32[4096]{0:T(1024)S(1)}, bf16[512,4096]{1,0:T(8,128)(2,1)}) fusion(f32[512,4096]{1,0:T(8,128)} %get-tuple-element.48, bf16[4096,1024]{1,0:T(8,128)(2,1)} %param.25, bf16[1,512,1024]{2,1,0:T(8,128)(2,1)S(1)} %copy-done.26, f32[512,4096]{1,0:T(8,128)} %get-tuple-element.74, f32[4096]{0:T(1024)S(1)} %convert_element_type.108), kind=kOutput, calls=%fused_computation.2 | convolution fusion | flops 4330614784 | bytes 30441472 | tf_op jit(solution)/shard_map/fd,kd->fk/dot_general | solution.py:52
  143.1 8.9 %multiply_reduce_fusion = (f32[1024]{0:T(1024)S(1)}, f32[512]{0:T(512)S(1)}, f32[512]{0:T(512)S(1)}, f32[512,1024]{1,0:T(8,128)S(1)}) fusion(f32[512,1024]{1,0:T(8,128)S(1)} %get-tuple-element.73, f32[512]{0:T(512)S(1)} %add_rsqrt_fusion, f32[512]{0:T(512)S(1)} %broadcast_multiply_fusion.4, f32[1024]{0:T(1024)S(1)} %convert_element_type.106, ...), kind=kOutput, calls=%fused_computation.43 | convolution fusion | flops 4299159552 | bytes 16793600 | tf_op jit(solution)/shard_map/fk,dk->fd/dot_general | solution.py:52
  152.1 0.8 convert_reduce_fusion.1
  153.0 1.3 copy-done.15
  154.3 1.3 convolution_convert_fusion.9
  156.2 0.9 dynamic-slice_bitcast_fusion.1
  157.2 10.4 %convolution_convert_fusion.1 = bf16[4096,1024]{1,0:T(8,128)(2,1)} fusion(bf16[512,4096]{1,0:T(8,128)(2,1)} %get-tuple-element.47, bf16[1,512,1024]{2,1,0:T(8,128)(2,1)} %param.27), kind=kOutput, calls=%fused_computation.19 | convolution fusion | flops 4299161600 | bytes 13631488 | tf_op jit(solution)/shard_map/fk,fd->kd/dot_general | solution.py:52
  167.6 9.0 %fusion.14 = bf16[1,512,1024]{2,1,0:T(8,128)(2,1)} fusion(f32[512,1024]{1,0:T(8,128)S(1)} %copy-done.14, bf16[512,4096]{1,0:T(8,128)(2,1)S(1)} %copy-done.45, bf16[4096,1024]{1,0:T(8,128)(2,1)} %param.25, f32[1024]{0:T(1024)S(1)} %convert_element_type.110), kind=kOutput, calls=%fused_computation.78 | convolution fusion | flops 4296540160 | bytes 15732736 | tf_op jit(solution)/shard_map/fk,kd->fd/dot_general | solution.py:52
  176.6 7.5 %convolution_convert_fusion = bf16[1024,4096]{1,0:T(8,128)(2,1)} fusion(bf16[512,4096]{1,0:T(8,128)(2,1)S(1)} %copy-done.46, f32[512,1024]{1,0:T(8,128)S(1)} %copy-done.14, f32[1024]{0:T(1024)S(1)} %convert_element_type.106, f32[512]{0:T(512)S(1)} %add_rsqrt_fusion, f32[512]{0:T(512)S(1)} %broadcast_multiply_fusion.4), kind=kOutput, calls=%fused_computation.18 | convolution fusion | flops 4301258752 | bytes 14688256 | tf_op jit(solution)/shard_map/fd,fk->dk/dot_general | solution.py:52
  184.3 0.8 copy-done.22
  185.1 2.9 fusion.40
  188.0 2.3 copy.59.grad
  190.3 1.6 bitcast_reduce_fusion
  191.9 1.2 copy-done.7
  193.1 1.2 copy-done.9
  194.3 29.9 %attend_back.1 = (bf16[1024,512]{1,0:T(8,128)(2,1)S(1)}, bf16[1792,1024]{1,0:T(8,128)(2,1)}) custom-call(s32[3,7]{1,0:T(4,128)S(1)} %pad_add_fusion.6.kspan, s32[3,2]{1,0:T(4,128)S(1)} %pad_add_fusion.7.qspan, f32[8]{0:T(128)S(1)} %exponential_multiply_fusion.slopes, bf16[1024,512]{1,0:T(8,128)(2,1)S(1)} %copy-done.6, bf16[512,1024]{1,0:T(8,128)(2,1)S(1)} %bitcast.98, ...), custom_call_target="tpu_custom_call" | custom-call | flops 20000000000 | bytes 16000000 | tf_op jit(solution)/shard_map/attend_back/pallas_call | solution.py:254
  224.2 3.3 convolution_convert_fusion.7
  228.1 2.7 convolution_convert_fusion.5
  230.7 2.3 fusion.7
  233.4 13.8 %collective-permute-start.7 = (bf16[384,1024]{1,0:T(8,128)(2,1)S(1)}, bf16[384,1024]{1,0:T(8,128)(2,1)S(1)}, u32[]{:S(2)}, u32[]{:S(2)}) collective-permute-start(bf16[384,1024]{1,0:T(8,128)(2,1)S(1)} %add_convert_fusion.3), channel_id=1, source_target_pairs={{0,2},{1,3},{2,0},{3,1},{4,6},{5,7},{6,4},{7,5},{8,10},{9,11},{10,... | collective-permute-start | bytes 2359304 | tf_op jit(solution)/shard_map/ppermute | solution.py:511
  247.2 2.7 convolution_add_fusion
  250.2 3.6 convolution_convert_fusion.8
  253.7 11.3 %collective-permute-done.7 = bf16[384,1024]{1,0:T(8,128)(2,1)S(1)} collective-permute-done((bf16[384,1024]{1,0:T(8,128)(2,1)S(1)}, bf16[384,1024]{1,0:T(8,128)(2,1)S(1)}, u32[]{:S(2)}, u32[]{:S(2)}) %collective-permute-start.7) | collective-permute-done | bytes 786464 | tf_op jit(solution)/shard_map/ppermute | solution.py:511
  265.1 6.7 %convolution_convert_fusion.6 = bf16[1024,1024]{1,0:T(8,128)(2,1)} fusion(bf16[1792,1024]{1,0:T(8,128)(2,1)S(1)} %copy-done.44, bf16[768,1024]{1,0:T(8,128)(2,1)S(1)} %copy-done.25, bf16[512,1024]{1,0:T(8,128)(2,1)} %collective-permute-done, bf16[512,1024]{1,0:T(8,128)(2,1)S(1)} %copy-done.19), kind=kOutput, calls=%fused_computation.59 | convolution fusion | flops 3770155008 | bytes 9437184 | tf_op jit(solution)/shard_map/fd,fe->de/dot_general | solution.py:52
  271.8 2.5 fusion.10
  274.4 2.3 multiply_reduce_fusion.1
  277.0 3.7 add_convert_fusion.1
  280.7 4.4 convolution_convert_fusion.2
  285.1 150.7 %share.1 = (f32[128,1024]{1,0:T(8,128)S(1)}, f32[32,4096]{1,0:T(8,128)S(1)}, f32[32,3072]{1,0:T(8,128)S(1)}, f32[32,1024]{1,0:T(8,128)S(1)}, f32[64,1024]{1,0:T(8,128)S(1)}, /*index=5*/f32[8,128]{1,0:T(8,128)S(1)}) custom-call(bf16[4,2,2,2,128,1024]{5,4,3,2,1,0:T(8,128)(2,1)} %bitcast.105, bf16[4,2,2,2,32,4096]{5,4,3,2,1,0:T(8,128)(2,1)} %bitcast.106, ...), custom_call_target="tpu_custom_call" | custom-call | flops 30000000 | bytes 60000000 | tf_op jit(solution)/shard_map/share/pallas_call | solution.py:474
  435.8 0.6 slice_bitcast_fusion.7
  436.9 2.4 convolution_convert_fusion.4
  439.3 1.5 slice_bitcast_fusion.2
  440.8 0.7 copy.73
  441.5 0.7 copy.74
  442.3 0.7 copy.75
  442.9 0.8 copy.76
  443.7 0.8 copy.77
  (153 shorter events, 6.2 us)
Async XLA Ops:
  0.6 98.4 %copy-start = (bf16[1024,1024]{1,0:T(8,128)(2,1)S(1)}, bf16[1024,1024]{1,0:T(8,128)(2,1)}, u32[]{:S(2)}) copy-start(bf16[1024,1024]{1,0:T(8,128)(2,1)} %param.21) | copy-start | bytes 6291460
  0.7 5.8 %copy-start.38 = (bf16[1024]{0:T(1024)(128)(2,1)S(1)}, bf16[1024]{0:T(1024)(128)(2,1)}, u32[]{:S(2)}) copy-start(bf16[1024]{0:T(1024)(128)(2,1)} %param.19) | copy-start | bytes 6148
  6.1 1.3 copy-start.10
  6.1 2.4 copy-start.35
  6.1 2.4 copy-start.36
  6.1 2.4 copy-start.31
  6.5 2.0 copy-start.33
  7.4 0.6 copy-start.29
  8.0 45.4 %copy-start.18 = (bf16[512,1024]{1,0:T(8,128)(2,1)}, bf16[512,1024]{1,0:T(8,128)(2,1)S(1)}, u32[]{:S(2)}) copy-start(bf16[512,1024]{1,0:T(8,128)(2,1)S(1)} %multiply_convert_fusion.2) | copy-start | bytes 3145732
  8.0 2.9 collective-permute-start
  13.9 20.4 %collective-permute-start.1 = (bf16[384,1024]{1,0:T(8,128)(2,1)}, bf16[384,1024]{1,0:T(8,128)(2,1)}, u32[]{:S(2)}, u32[]{:S(2)}) collective-permute-start(bf16[384,1024]{1,0:T(8,128)(2,1)} %fusion.24), channel_id=1, source_target_pairs={{0,2},{1,3},{2,0},{3,1},{4,6},{5,7},{6,4},{7,5},{8,10},{9,11},{10,... | collective-permute-start | bytes 2359304 | tf_op jit(solution)/shard_map/ppermute | solution.py:511
  34.3 16.1 %collective-permute-start.2 = (bf16[384,1024]{1,0:T(8,128)(2,1)}, bf16[384,1024]{1,0:T(8,128)(2,1)}, u32[]{:S(2)}, u32[]{:S(2)}) collective-permute-start(bf16[384,1024]{1,0:T(8,128)(2,1)} %collective-permute-done.1), channel_id=1, source_target_pairs={{0,1},{1,0},{2,3},{3,2},{4,5},{5,4},{6,7},{7,6},{8,9},{9,8},{10,11... | collective-permute-start | bytes 2359304 | tf_op jit(solution)/shard_map/ppermute | solution.py:507
  39.1 7.1 %copy-start.39 = (bf16[1024]{0:T(1024)(128)(2,1)S(1)}, bf16[1024]{0:T(1024)(128)(2,1)}, u32[]{:S(2)}) copy-start(bf16[1024]{0:T(1024)(128)(2,1)} %param.22) | copy-start | bytes 6148
  42.2 4.0 copy-start.37
  42.2 4.1 copy-start.40
  50.3 3.0 copy-start.20
  53.3 5.8 %copy-start.24 = (bf16[768,1024]{1,0:T(8,128)(2,1)}, bf16[768,1024]{1,0:T(8,128)(2,1)S(1)}, u32[]{:S(2)}) copy-start(bf16[768,1024]{1,0:T(8,128)(2,1)S(1)} %fusion.12) | copy-start | bytes 4718596
  59.2 1.8 copy-start.12
  69.2 22.5 %copy-start.8 = (s32[1792,128]{1,0:T(8,128)}, s32[1792,128]{1,0:T(8,128)S(1)}, u32[]{:S(2)}) copy-start(s32[1792,128]{1,0:T(8,128)S(1)} %broadcast_in_dim.97.kcode) | copy-start | bytes 2752516
  69.2 2.4 copy-start.2
  71.6 1.5 copy-start.3
  73.1 1.2 copy-start.4
  92.8 4.4 collective-permute-start.3
  97.1 5.7 %slice-start = ((s8[8388608]{0:T(1024)(128)(4,1)}), s8[4194304]{0:T(1024)(128)(4,1)S(1)}, s32[]{:S(2)}) async-start(s8[8388608]{0:T(1024)(128)(4,1)} %bitcast.133), calls=%async_computation | async-start | bytes 8388608
  99.1 3.4 copy-start.27
  99.1 3.7 slice-start.1
  102.4 49.7 %copy-start.13 = (f32[512,1024]{1,0:T(8,128)}, f32[512,1024]{1,0:T(8,128)S(1)}, u32[]{:S(2)}) copy-start(f32[512,1024]{1,0:T(8,128)S(1)} %get-tuple-element.73) | copy-start | bytes 6291460
  102.8 25.6 %copy-start.26 = (bf16[1,512,1024]{2,1,0:T(8,128)(2,1)S(1)}, bf16[1,512,1024]{2,1,0:T(8,128)(2,1)}, u32[]{:S(2)}) copy-start(bf16[1,512,1024]{2,1,0:T(8,128)(2,1)} %param.27) | copy-start | bytes 3145732
  153.0 1.3 copy-start.15
  157.0 27.3 %collective-permute-start.4 = (bf16[512,512]{0,1:T(8,128)(2,1)S(1)}, bf16[512,512]{0,1:T(8,128)(2,1)S(1)}, u32[]{:S(2)}, u32[]{:S(2)}) collective-permute-start(bf16[512,512]{0,1:T(8,128)(2,1)S(1)} %get-tuple-element.58), channel_id=1, source_target_pairs={{0,1},{1,0},{2,3},{3,2},{4,5},{5,4},{6,7},{7,6},{8,9},{9,8},{10,11... | collective-permute-start | bytes 1572872 | tf_op jit(solution)/shard_map/ppermute | solution.py:507
  157.2 10.4 %copy-start.14 = (f32[512,1024]{1,0:T(8,128)S(1)}, f32[512,1024]{1,0:T(8,128)}, u32[]{:S(2)}) copy-start(f32[512,1024]{1,0:T(8,128)} %copy-done.13) | copy-start | bytes 6291460
  157.2 10.4 %copy-start.45 = (bf16[512,4096]{1,0:T(8,128)(2,1)S(1)}, bf16[512,4096]{1,0:T(8,128)(2,1)}, u32[]{:S(2)}) copy-start(bf16[512,4096]{1,0:T(8,128)(2,1)} %get-tuple-element.47) | copy-start | bytes 12582916
  167.6 9.0 %copy-start.46 = (bf16[512,4096]{1,0:T(8,128)(2,1)S(1)}, bf16[512,4096]{1,0:T(8,128)(2,1)}, u32[]{:S(2)}) copy-start(bf16[512,4096]{1,0:T(8,128)(2,1)} %get-tuple-element.77) | copy-start | bytes 12582916
  184.1 6.2 %copy-start.17 = (bf16[512,512]{0,1:T(8,128)(2,1)S(1)}, bf16[512,512]{0,1:T(8,128)(2,1)}, u32[]{:S(2)}) copy-start(bf16[512,512]{0,1:T(8,128)(2,1)} %get-tuple-element.57) | copy-start | bytes 1572868
  184.3 0.8 copy-start.22
  185.1 5.2 %copy-start.23 = (bf16[512,512]{0,1:T(8,128)(2,1)S(1)}, bf16[512,512]{0,1:T(8,128)(2,1)}, u32[]{:S(2)}) copy-start(bf16[512,512]{0,1:T(8,128)(2,1)} %copy-done.22) | copy-start | bytes 1572868
  185.1 6.8 %copy-start.5 = (bf16[1024,512]{0,1:T(8,128)(2,1)S(1)}, bf16[1024,512]{0,1:T(8,128)(2,1)}, u32[]{:S(2)}) copy-start(bf16[1024,512]{0,1:T(8,128)(2,1)} %convolution_convert_fusion.10) | copy-start | bytes 3145732
  185.1 6.8 %copy-start.6 = (bf16[1024,512]{1,0:T(8,128)(2,1)S(1)}, bf16[1024,512]{1,0:T(8,128)(2,1)}, u32[]{:S(2)}) copy-start(bf16[1024,512]{1,0:T(8,128)(2,1)} %copy.57.q) | copy-start | bytes 3145732
  191.9 1.2 copy-start.7
  193.1 1.2 copy-start.9
  194.3 29.9 %copy-start.21 = (bf16[1024,2,512]{0,2,1:T(8,128)(2,1)S(1)}, bf16[1024,2,512]{0,2,1:T(8,128)(2,1)}, u32[]{:S(2)}) copy-start(bf16[1024,2,512]{0,2,1:T(8,128)(2,1)} %copy.51) | copy-start | bytes 6291460
  224.2 3.9 copy-start.16
  224.2 3.9 copy-start.28
  227.6 3.1 copy-start.44
  227.6 5.4 %collective-permute-start.6 = (bf16[384,1024]{1,0:T(8,128)(2,1)S(1)}, bf16[384,1024]{1,0:T(8,128)(2,1)S(1)}, u32[]{:S(2)}, u32[]{:S(2)}) collective-permute-start(bf16[384,1024]{1,0:T(8,128)(2,1)S(1)} %constant_dynamic-slice_fusion), channel_id=1, source_target_pairs={{0,1},{1,0},{2,3},{3,2},{4,5},{5,4},{6,7},{7,6},{8,9},{9,8},{10,11... | collective-permute-start | bytes 2359304 | tf_op jit(solution)/shard_map/ppermute | solution.py:507
  233.4 31.7 %collective-permute-start.7 = (bf16[384,1024]{1,0:T(8,128)(2,1)S(1)}, bf16[384,1024]{1,0:T(8,128)(2,1)S(1)}, u32[]{:S(2)}, u32[]{:S(2)}) collective-permute-start(bf16[384,1024]{1,0:T(8,128)(2,1)S(1)} %add_convert_fusion.3), channel_id=1, source_target_pairs={{0,2},{1,3},{2,0},{3,1},{4,6},{5,7},{6,4},{7,5},{8,10},{9,11},{10,... | collective-permute-start | bytes 2359304 | tf_op jit(solution)/shard_map/ppermute | solution.py:511
  247.2 2.9 copy-start.19
  250.1 15.0 %copy-start.25 = (bf16[768,1024]{1,0:T(8,128)(2,1)S(1)}, bf16[768,1024]{1,0:T(8,128)(2,1)}, u32[]{:S(2)}) copy-start(bf16[768,1024]{1,0:T(8,128)(2,1)} %copy-done.24) | copy-start | bytes 4718596
  250.1 24.3 %collective-permute-start.5 = (bf16[512,1024]{1,0:T(8,128)(2,1)S(1)}, bf16[512,1024]{1,0:T(8,128)(2,1)S(1)}, u32[]{:S(2)}, u32[]{:S(2)}) collective-permute-start(bf16[512,1024]{1,0:T(8,128)(2,1)S(1)} %slice.164), channel_id=1, source_target_pairs={{0,1},{1,0},{2,3},{3,2},{4,5},{5,4},{6,7},{7,6},{8,9},{9,8},{10,11... | collective-permute-start | bytes 3145736 | tf_op jit(solution)/shard_map/ppermute | solution.py:507
  265.0 6.8 %collective-permute-start.8 = (bf16[384,1024]{1,0:T(8,128)(2,1)S(1)}, bf16[384,1024]{1,0:T(8,128)(2,1)S(1)}, u32[]{:S(2)}, u32[]{:S(2)}) collective-permute-start(bf16[384,1024]{1,0:T(8,128)(2,1)S(1)} %collective-permute-done.7), channel_id=1, source_target_pairs={{0,1},{1,0},{2,3},{3,2},{4,5},{5,4},{6,7},{7,6},{8,9},{9,8},{10,11... | collective-permute-start | bytes 2359304 | tf_op jit(solution)/shard_map/ppermute | solution.py:507
  271.8 2.6 copy-start.11
  271.8 2.6 copy-start.30
  271.8 2.6 copy-start.32
  271.8 2.6 copy-start.34
  277.0 3.7 copy-start.42
  277.0 3.7 copy-start.43
  285.1 151.8 %copy-start.41 = (bf16[2048,1024]{1,0:T(8,128)(2,1)S(1)}, bf16[2048,1024]{1,0:T(8,128)(2,1)}, u32[]{:S(2)}) copy-start(bf16[2048,1024]{1,0:T(8,128)(2,1)} %param.18) | copy-start | bytes 12582916
  439.3 5.2 %copy-start.1 = (bf16[1024,1024]{1,0:T(8,128)(2,1)S(1)}, bf16[1024,1024]{1,0:T(8,128)(2,1)}, u32[]{:S(2)}) copy-start(bf16[1024,1024]{1,0:T(8,128)(2,1)} %param.21) | copy-start | bytes 6291460
